TPU v7x, 256 devices: a whole 4x4x8 slice. The times are simulated.
256 devices in a mesh: pipe: 4 (over y_hi, core), section: 8 (over y_lo, x), tp: 8 (over z).
Axes of the slice: x: 4, y: 4 (y_hi: 2, y_lo: 2; y = y_hi * 2 + y_lo), z: 8, core: 2. Of those that a mesh axis runs over, the one named last changes fastest.
Arguments:
- weights: bfloat16 [4, 8, 2, 4096, 512], P('pipe', 'section', None, 'tp'), may hold values from -6 to 6
- first_moment: float32 [4, 8, 2, 4096, 512], P('pipe', 'section', None, 'tp'), may hold values from -4 to 4
- second_moment: float32 [4, 8, 2, 4096, 512], P('pipe', 'section', None, 'tp'), may hold values from 0.1 to 2
- gradients: bfloat16 [4, 8, 2, 4096, 512], P('pipe', 'section', None, 'tp'), may hold values from -6 to 6
- old_section: int32 [4, 12], replicated, may hold values from 0 to 7, as said below
- new_section: int32 [12], replicated, may hold values from 0 to 7, as said below
- lost_pipe: int32 [4], replicated, may hold values from 0 to 3, each once
- donor_offset: int32 [12], replicated, may hold values from 1 to 3
Outputs:
- new_weights: bfloat16 [4, 8, 2, 4096, 512], P('pipe', 'section', None, 'tp')
- new_first: float32 [4, 8, 2, 4096, 512], P('pipe', 'section', None, 'tp')
- new_second: float32 [4, 8, 2, 4096, 512], P('pipe', 'section', None, 'tp')
Inputs may be any that keep to these rules, and one draw needn't show every extreme that they name: `old_section`: each row places layers in section order (a layer's section never falls with the layer); 4 sections of each row hold exactly 2 layers and the others one each. `new_section`: layers in any order; no section holds more than 2 layers, and some section holds exactly 2.
All inputs are finite; a program needn't handle non-finite values.
Results may differ from a plain program's by a relative error of at most 0.0075.
Values may be sent and summed in bfloat16 or wider, within the bound.
A program may use at most 64 MiB of HBM per device.

v0:
```python
import jax
import jax.numpy as jnp
from jax import lax
from jax.sharding import PartitionSpec as P

LEARN_RATE = 0.01
BETA_ONE = 0.9
BETA_TWO = 0.95
EPSILON = 1e-08
DECAY_RATE = 0.1


def slot_ranks(section_map):
    layer_ids = jnp.arange(section_map.shape[-1], dtype=jnp.int32)
    same_section = section_map[..., :, None] == section_map[..., None, :]
    before = layer_ids[None, :] < layer_ids[:, None]
    return jnp.sum((same_section & before).astype(jnp.int32), axis=-1)


def per_device(
    weights,
    first_moment,
    second_moment,
    gradients,
    old_section,
    new_section,
    lost_pipe,
    donor_offset,
):
    pipe_total = lax.axis_size("pipe")
    section_total = lax.axis_size("section")
    slot_count = weights.shape[2]
    layer_count = new_section.shape[0]
    held_state = (weights[0, 0], first_moment[0, 0], second_moment[0, 0], gradients[0, 0])
    spread = (
        lax.all_to_all(held_state[0], ("pipe", "section"), split_axis=1, concat_axis=0, tiled=True),
        lax.all_to_all(
            held_state[1].astype(jnp.bfloat16),
            ("pipe", "section"),
            split_axis=1,
            concat_axis=0,
            tiled=True,
        ).astype(jnp.float32),
        lax.all_to_all(
            held_state[2].astype(jnp.bfloat16),
            ("pipe", "section"),
            split_axis=1,
            concat_axis=0,
            tiled=True,
        ).astype(jnp.float32),
        lax.all_to_all(held_state[3], ("pipe", "section"), split_axis=1, concat_axis=0, tiled=True),
    )
    piece_weight, piece_one, piece_two, piece_grad = spread

    def incoming(pipe_at, section_at, slot_at):
        return (pipe_at * section_total + section_at) * slot_count + slot_at

    pipe_ids = jnp.arange(pipe_total, dtype=jnp.int32)
    layer_ids = jnp.arange(layer_count, dtype=jnp.int32)
    is_lost = pipe_ids == lost_pipe[0]
    now_section = jnp.where(is_lost[:, None], new_section[None, :], old_section)
    now_slot = slot_ranks(now_section)
    old_slot = slot_ranks(old_section)
    donors = lost_pipe[donor_offset]
    source = jnp.where(is_lost[:, None], donors[None, :], pipe_ids[:, None])
    source_section = old_section[source, layer_ids[None, :]]
    source_slot = old_slot[source, layer_ids[None, :]]
    grad_index = incoming(pipe_ids[:, None], now_section, now_slot)
    grad_rows = piece_grad[grad_index].astype(jnp.float32)
    mean_grad = jnp.sum(grad_rows, axis=0) / pipe_total
    source_index = incoming(source, source_section, source_slot)
    weight_now = piece_weight[source_index].astype(jnp.float32)
    moment_one = piece_one[source_index]
    moment_two = piece_two[source_index]
    next_one = BETA_ONE * moment_one + (1.0 - BETA_ONE) * mean_grad[None]
    next_two = BETA_TWO * moment_two + (1.0 - BETA_TWO) * mean_grad[None] * mean_grad[None]
    update = next_one / (jnp.sqrt(next_two) + EPSILON) + DECAY_RATE * weight_now
    next_weight = (weight_now - LEARN_RATE * update).astype(jnp.bfloat16)
    place_index = (pipe_ids[:, None] * section_total + now_section) * slot_count + now_slot
    out_weight = jnp.zeros(piece_weight.shape, jnp.bfloat16).at[place_index].set(next_weight)
    out_one = jnp.zeros(piece_one.shape, jnp.float32).at[place_index].set(next_one)
    out_two = jnp.zeros(piece_two.shape, jnp.float32).at[place_index].set(next_two)
    returned = (
        lax.all_to_all(out_weight, ("pipe", "section"), split_axis=0, concat_axis=1, tiled=True),
        lax.all_to_all(
            out_one.astype(jnp.bfloat16),
            ("pipe", "section"),
            split_axis=0,
            concat_axis=1,
            tiled=True,
        ).astype(out_one.dtype),
        lax.all_to_all(
            out_two.astype(jnp.bfloat16),
            ("pipe", "section"),
            split_axis=0,
            concat_axis=1,
            tiled=True,
        ).astype(out_two.dtype),
    )
    final_weight, final_one, final_two = returned
    return (final_weight[None, None], final_one[None, None], final_two[None, None])


def solution(mesh):
    in_specs = (
        P("pipe", "section", None, "tp", None),
        P("pipe", "section", None, "tp", None),
        P("pipe", "section", None, "tp", None),
        P("pipe", "section", None, "tp", None),
        P(),
        P(),
        P(),
        P(),
    )
    out_specs = (
        P("pipe", "section", None, "tp", None),
        P("pipe", "section", None, "tp", None),
        P("pipe", "section", None, "tp", None),
    )
    return jax.shard_map(
        per_device, mesh=mesh, in_specs=in_specs, out_specs=out_specs, check_vma=False
    )
```

profile of v0, /device:TPU:1, one launch (start us, length us, event | category | flops | bytes accessed | tf_op | source)
XLA Modules:
  0.0 172.1 jit_solution(12032110834322884188)
XLA Ops:
  0.6 1.7 %convert_element_type.136 = bf16[1,1,2,512,512]{4,3,2,1,0:T(8,128)(2,1)S(1)} convert(f32[1,1,2,512,512]{4,3,2,1,0:T(8,128)} %param.9) | non-fusion elementwise | flops 524288 | bytes 3145728 | tf_op jit(solution)/shard_map/convert_element_type | solution.py:38
  2.4 2.0 %copy.79 = bf16[1,1,2,512,512]{4,2,3,1,0:T(2,128)(2,1)} copy(bf16[1,1,2,512,512]{4,3,2,1,0:T(8,128)(2,1)S(1)} %convert_element_type.136) | data formatting | bytes 2097152
  4.4 8.6 %all-to-all-start.1 = ((bf16[2,512,512]{2,0,1:T(2,128)(2,1)}), bf16[2,512,512]{2,0,1:T(2,128)(2,1)S(1)}, u32[]{:S(2)}, u32[]{:S(2)}) async-start(bf16[2,512,512]{2,0,1:T(2,128)(2,1)} %bitcast.55), calls=%async_computation.1 | async-start | bytes 2097152 | tf_op jit(solution)/shard_map/all_to_all | solution.py:37
  13.0 1.7 %convert_element_type.137 = bf16[1,1,2,512,512]{4,3,2,1,0:T(8,128)(2,1)S(1)} convert(f32[1,1,2,512,512]{4,3,2,1,0:T(8,128)} %param.10) | non-fusion elementwise | flops 524288 | bytes 3145728 | tf_op jit(solution)/shard_map/convert_element_type | solution.py:45
  14.7 2.0 %copy.78 = bf16[1,1,2,512,512]{4,2,3,1,0:T(2,128)(2,1)} copy(bf16[1,1,2,512,512]{4,3,2,1,0:T(8,128)(2,1)S(1)} %convert_element_type.137) | data formatting | bytes 2097152
  16.8 13.5 %all-to-all-done.1 = bf16[2,512,512]{2,0,1:T(2,128)(2,1)S(1)} async-done(((bf16[2,512,512]{2,0,1:T(2,128)(2,1)}), bf16[2,512,512]{2,0,1:T(2,128)(2,1)S(1)}, u32[]{:S(2)}, u32[]{:S(2)}) %all-to-all-start.1) | async-done | bytes 1048608 | tf_op jit(solution)/shard_map/all_to_all | solution.py:37
  30.3 3.7 %all-to-all-start.3 = ((bf16[2,512,512]{2,0,1:T(2,128)(2,1)}), bf16[2,512,512]{2,0,1:T(2,128)(2,1)S(1)}, u32[]{:S(2)}, u32[]{:S(2)}) async-start(bf16[2,512,512]{2,0,1:T(2,128)(2,1)} %bitcast.72), calls=%async_computation.3 | async-start | bytes 2097152 | tf_op jit(solution)/shard_map/all_to_all | solution.py:44
  34.0 0.1 copy.53
  34.3 0.1 copy.54
  34.4 0.7 gather_fusion
  35.1 0.1 reshape.229
  35.2 1.1 gather_fusion.1
  36.3 3.3 %copy.81 = bf16[1,1,2,512,512]{4,2,3,1,0:T(2,128)(2,1)} copy(bf16[1,1,2,512,512]{4,3,2,1,0:T(8,128)(2,1)} %param.8) | data formatting | bytes 2097152 | tf_op args[0]
  39.6 11.8 %all-to-all-done.3 = bf16[2,512,512]{2,0,1:T(2,128)(2,1)S(1)} async-done(((bf16[2,512,512]{2,0,1:T(2,128)(2,1)}), bf16[2,512,512]{2,0,1:T(2,128)(2,1)S(1)}, u32[]{:S(2)}, u32[]{:S(2)}) %all-to-all-start.3) | async-done | bytes 1048608 | tf_op jit(solution)/shard_map/all_to_all | solution.py:44
  51.4 4.5 %all-to-all-start = ((bf16[2,512,512]{2,0,1:T(2,128)(2,1)}), bf16[2,512,512]{2,0,1:T(2,128)(2,1)}, u32[]{:S(2)}, u32[]{:S(2)}) async-start(bf16[2,512,512]{2,0,1:T(2,128)(2,1)} %bitcast.70), calls=%async_computation | async-start | bytes 2097152 | tf_op jit(solution)/shard_map/all_to_all | solution.py:36
  55.9 0.5 convert_reduce_fusion.1
  56.4 1.0 gather_fusion.2
  57.6 0.1 reshape.243
  57.8 0.1 copy.55
  57.9 0.1 reshape.275
  58.0 3.3 %copy.80 = bf16[1,1,2,512,512]{4,2,3,1,0:T(2,128)(2,1)} copy(bf16[1,1,2,512,512]{4,3,2,1,0:T(8,128)(2,1)} %param.11) | data formatting | bytes 2097152 | tf_op args[3]
  61.3 0.2 copy.61
  61.5 11.7 %all-to-all-done = bf16[2,512,512]{2,0,1:T(2,128)(2,1)} async-done(((bf16[2,512,512]{2,0,1:T(2,128)(2,1)}), bf16[2,512,512]{2,0,1:T(2,128)(2,1)}, u32[]{:S(2)}, u32[]{:S(2)}) %all-to-all-start) | async-done | bytes 1048608 | tf_op jit(solution)/shard_map/all_to_all | solution.py:36
  73.2 4.6 %all-to-all-start.2 = ((bf16[2,512,512]{2,0,1:T(2,128)(2,1)}), bf16[2,512,512]{2,0,1:T(2,128)(2,1)}, u32[]{:S(2)}, u32[]{:S(2)}) async-start(bf16[2,512,512]{2,0,1:T(2,128)(2,1)} %bitcast.71), calls=%async_computation.2 | async-start | bytes 2097152 | tf_op jit(solution)/shard_map/all_to_all | solution.py:51
  77.9 0.3 convert_bitcast_fusion.3
  78.1 0.2 copy.62
  78.3 0.2 copy.67
  78.5 0.3 convert_bitcast_fusion.2
  78.8 1.6 copy.68
  80.4 1.8 %gather_fusion.4 = f32[48,16,512]{2,1,0:T(8,128)} fusion(f32[64,16,512]{2,1,0:T(8,128)S(1)} %bitcast.60, s32[1024]{0:T(1024)S(1)} %pad_clamp_fusion.1), kind=kCustom, calls=%fused_computation.4 | custom fusion | bytes 3145920 | tf_op jit(solution)/shard_map/gather | solution.py:73
  82.2 2.2 %gather_fusion.6 = f32[48,16,512]{2,1,0:T(8,128)S(1)} fusion(f32[64,16,512]{2,1,0:T(8,128)} %bitcast.61, s32[1024]{0:T(1024)S(1)} %pad_clamp_fusion.1), kind=kCustom, calls=%fused_computation.6 | custom fusion | bytes 3145920 | tf_op jit(solution)/shard_map/gather | solution.py:74
  84.4 1.4 copy.57
  85.8 1.1 copy.58
  86.9 2.7 %gather_fusion.3 = bf16[48,16,512]{2,1,0:T(8,128)(2,1)} fusion(bf16[64,16,512]{2,1,0:T(8,128)(2,1)} %bitcast.76, s32[1024]{0:T(1024)S(1)} %pad_clamp_fusion.1), kind=kCustom, calls=%fused_computation.3 | custom fusion | bytes 1573056 | tf_op jit(solution)/shard_map/gather | solution.py:72
  89.6 1.3 broadcast_multiply_fusion.1
  91.0 0.3 broadcast_multiply_fusion
  91.3 3.7 %all-to-all-done.2 = bf16[2,512,512]{2,0,1:T(2,128)(2,1)} async-done(((bf16[2,512,512]{2,0,1:T(2,128)(2,1)}), bf16[2,512,512]{2,0,1:T(2,128)(2,1)}, u32[]{:S(2)}, u32[]{:S(2)}) %all-to-all-start.2) | async-done | bytes 1048608 | tf_op jit(solution)/shard_map/all_to_all | solution.py:51
  95.0 1.4 copy.64
  96.4 0.1 copy.65
  96.5 0.6 gather_fusion.5
  97.2 0.1 convert_reduce_fusion
  97.3 0.1 broadcast_multiply_fusion.2
  97.4 1.1 copy-done.3
  98.6 0.2 copy-done.4
  98.8 2.5 %fusion.2 = (bf16[4,12,16,512]{3,2,1,0:T(8,128)(2,1)}, f32[4,12,16,512]{3,2,1,0:T(8,128)}, f32[4,12,16,512]{3,2,1,0:T(8,128)}) fusion(bf16[4,12,16,512]{3,2,1,0:T(8,128)(2,1)S(1)} %bitcast.78, f32[4,12,16,512]{3,2,1,0:T(8,128)S(1)} %bitcast.63, f32[12,16,512]{2,1,0:T(8,128)S(1)} %get-tuple-element.9, f32[4,12,16,512]{3,2,1,0:T(8,128)S(1)} %bitcast.62, ...), kind=kLoop, calls=%fused_computation.18 | loop fusion | flops 3932160 | bytes 8650752 | tf_op jit(solution)/shard_map/convert_element_type | solution.py:78
  101.3 0.2 broadcast.197.clone
  101.5 5.1 %scatter_fusion.1 = f32[64,16,512]{2,1,0:T(8,128)S(1)} fusion(f32[64,16,512]{2,1,0:T(8,128)S(1)} %broadcast.197.clone, s32[48]{0:T(128)S(1)} %reshape.275, f32[48,16,512]{2,1,0:T(8,128)} %bitcast.65), kind=kCustom, calls=%fused_computation.8 | custom fusion | bytes 4718784 | tf_op jit(solution)/shard_map/scatter | solution.py:81
  106.7 1.1 convert_element_type.112
  107.8 3.7 %all-to-all-start.5 = ((bf16[64,16,512]{2,1,0:T(8,128)(2,1)}), bf16[64,16,512]{2,1,0:T(8,128)(2,1)S(1)}, u32[]{:S(2)}, u32[]{:S(2)}) async-start(bf16[64,16,512]{2,1,0:T(8,128)(2,1)} %convert_element_type.112), calls=%async_computation.5 | async-start | bytes 2097152 | tf_op jit(solution)/shard_map/all_to_all | solution.py:85
  111.5 0.2 broadcast.197.clone.1
  111.8 5.1 %scatter_fusion.2 = f32[64,16,512]{2,1,0:T(8,128)S(1)} fusion(f32[64,16,512]{2,1,0:T(8,128)S(1)} %broadcast.197.clone.1, s32[48]{0:T(128)S(1)} %reshape.275, f32[48,16,512]{2,1,0:T(8,128)} %bitcast.64), kind=kCustom, calls=%fused_computation.9 | custom fusion | bytes 4718784 | tf_op jit(solution)/shard_map/scatter | solution.py:82
  116.9 1.1 convert_element_type.117
  118.0 10.9 %all-to-all-done.5 = bf16[64,16,512]{2,1,0:T(8,128)(2,1)S(1)} async-done(((bf16[64,16,512]{2,1,0:T(8,128)(2,1)}), bf16[64,16,512]{2,1,0:T(8,128)(2,1)S(1)}, u32[]{:S(2)}, u32[]{:S(2)}) %all-to-all-start.5) | async-done | bytes 1048608 | tf_op jit(solution)/shard_map/all_to_all | solution.py:85
  128.9 3.7 %all-to-all-start.6 = ((bf16[64,16,512]{2,1,0:T(8,128)(2,1)}), bf16[64,16,512]{2,1,0:T(8,128)(2,1)S(1)}, u32[]{:S(2)}, u32[]{:S(2)}) async-start(bf16[64,16,512]{2,1,0:T(8,128)(2,1)} %convert_element_type.117), calls=%async_computation.6 | async-start | bytes 2097152 | tf_op jit(solution)/shard_map/all_to_all | solution.py:92
  132.6 1.1 broadcast_in_dim.50
  133.7 6.2 %scatter_fusion = bf16[64,16,512]{2,1,0:T(8,128)(2,1)} fusion(bf16[64,16,512]{2,1,0:T(8,128)(2,1)} %broadcast_in_dim.50, s32[48]{0:T(128)S(1)} %reshape.275, bf16[48,16,512]{2,1,0:T(8,128)(2,1)S(1)} %bitcast.79), kind=kCustom, calls=%fused_computation.7 | custom fusion | bytes 2359488 | tf_op jit(solution)/shard_map/scatter | solution.py:80
  140.0 10.0 %all-to-all-done.6 = bf16[64,16,512]{2,1,0:T(8,128)(2,1)S(1)} async-done(((bf16[64,16,512]{2,1,0:T(8,128)(2,1)}), bf16[64,16,512]{2,1,0:T(8,128)(2,1)S(1)}, u32[]{:S(2)}, u32[]{:S(2)}) %all-to-all-start.6) | async-done | bytes 1048608 | tf_op jit(solution)/shard_map/all_to_all | solution.py:92
  150.0 3.7 %all-to-all-start.4 = ((bf16[64,16,512]{2,1,0:T(8,128)(2,1)}), bf16[64,16,512]{2,1,0:T(8,128)(2,1)S(1)}, u32[]{:S(2)}, u32[]{:S(2)}) async-start(bf16[64,16,512]{2,1,0:T(8,128)(2,1)} %scatter_fusion), calls=%async_computation.4 | async-start | bytes 2097152 | tf_op jit(solution)/shard_map/all_to_all | solution.py:84
  153.7 0.3 convert_bitcast_fusion.1
  154.0 1.6 copy.70
  155.6 0.3 convert_bitcast_fusion
  155.8 1.6 copy.71
  157.4 13.7 %all-to-all-done.4 = bf16[64,16,512]{2,1,0:T(8,128)(2,1)S(1)} async-done(((bf16[64,16,512]{2,1,0:T(8,128)(2,1)}), bf16[64,16,512]{2,1,0:T(8,128)(2,1)S(1)}, u32[]{:S(2)}, u32[]{:S(2)}) %all-to-all-start.4) | async-done | bytes 1048608 | tf_op jit(solution)/shard_map/all_to_all | solution.py:84
  171.1 1.1 copy.69
  (27 shorter events, 0.6 us)
Async XLA Ops:
  4.4 25.9 %all-to-all-start.1 = ((bf16[2,512,512]{2,0,1:T(2,128)(2,1)}), bf16[2,512,512]{2,0,1:T(2,128)(2,1)S(1)}, u32[]{:S(2)}, u32[]{:S(2)}) async-start(bf16[2,512,512]{2,0,1:T(2,128)(2,1)} %bitcast.55), calls=%async_computation.1 | async-start | bytes 2097152 | tf_op jit(solution)/shard_map/all_to_all | solution.py:37
  16.8 17.3 %copy-start = (s32[4,12]{1,0:T(4,128)S(1)}, s32[4,12]{1,0:T(4,128)}, u32[]{:S(2)}) copy-start(s32[4,12]{1,0:T(4,128)} %param.12) | copy-start | bytes 580
  16.8 17.4 %copy-start.1 = (s32[4]{0:T(128)S(1)}, s32[4]{0:T(128)}, u32[]{:S(2)}) copy-start(s32[4]{0:T(128)} %param.14) | copy-start | bytes 52
  16.8 17.4 %copy-start.6 = (s32[12]{0:T(128)S(1)}, s32[12]{0:T(128)}, u32[]{:S(2)}) copy-start(s32[12]{0:T(128)} %param.13) | copy-start | bytes 148
  16.8 17.6 %copy-start.7 = (s32[12]{0:T(128)S(1)}, s32[12]{0:T(128)}, u32[]{:S(2)}) copy-start(s32[12]{0:T(128)} %param.15) | copy-start | bytes 148
  30.3 21.1 %all-to-all-start.3 = ((bf16[2,512,512]{2,0,1:T(2,128)(2,1)}), bf16[2,512,512]{2,0,1:T(2,128)(2,1)S(1)}, u32[]{:S(2)}, u32[]{:S(2)}) async-start(bf16[2,512,512]{2,0,1:T(2,128)(2,1)} %bitcast.72), calls=%async_computation.3 | async-start | bytes 2097152 | tf_op jit(solution)/shard_map/all_to_all | solution.py:44
  51.4 21.8 %all-to-all-start = ((bf16[2,512,512]{2,0,1:T(2,128)(2,1)}), bf16[2,512,512]{2,0,1:T(2,128)(2,1)}, u32[]{:S(2)}, u32[]{:S(2)}) async-start(bf16[2,512,512]{2,0,1:T(2,128)(2,1)} %bitcast.70), calls=%async_computation | async-start | bytes 2097152 | tf_op jit(solution)/shard_map/all_to_all | solution.py:36
  73.2 21.8 %all-to-all-start.2 = ((bf16[2,512,512]{2,0,1:T(2,128)(2,1)}), bf16[2,512,512]{2,0,1:T(2,128)(2,1)}, u32[]{:S(2)}, u32[]{:S(2)}) async-start(bf16[2,512,512]{2,0,1:T(2,128)(2,1)} %bitcast.71), calls=%async_computation.2 | async-start | bytes 2097152 | tf_op jit(solution)/shard_map/all_to_all | solution.py:51
  85.8 3.8 %copy-start.2 = (f32[48,16,512]{2,1,0:T(8,128)S(1)}, f32[48,16,512]{2,1,0:T(8,128)}, u32[]{:S(2)}) copy-start(f32[48,16,512]{2,1,0:T(8,128)} %gather_fusion.4) | copy-start | bytes 4718596
  97.1 1.4 copy-start.3
  97.2 1.6 copy-start.4
  107.8 21.1 %all-to-all-start.5 = ((bf16[64,16,512]{2,1,0:T(8,128)(2,1)}), bf16[64,16,512]{2,1,0:T(8,128)(2,1)S(1)}, u32[]{:S(2)}, u32[]{:S(2)}) async-start(bf16[64,16,512]{2,1,0:T(8,128)(2,1)} %convert_element_type.112), calls=%async_computation.5 | async-start | bytes 2097152 | tf_op jit(solution)/shard_map/all_to_all | solution.py:85
  118.0 15.7 %copy-start.5 = (bf16[4,12,16,512]{3,2,1,0:T(8,128)(2,1)S(1)}, bf16[4,12,16,512]{3,2,1,0:T(8,128)(2,1)}, u32[]{:S(2)}) copy-start(bf16[4,12,16,512]{3,2,1,0:T(8,128)(2,1)} %get-tuple-element.5) | copy-start | bytes 2359300
  128.9 21.1 %all-to-all-start.6 = ((bf16[64,16,512]{2,1,0:T(8,128)(2,1)}), bf16[64,16,512]{2,1,0:T(8,128)(2,1)S(1)}, u32[]{:S(2)}, u32[]{:S(2)}) async-start(bf16[64,16,512]{2,1,0:T(8,128)(2,1)} %convert_element_type.117), calls=%async_computation.6 | async-start | bytes 2097152 | tf_op jit(solution)/shard_map/all_to_all | solution.py:92
  150.0 21.1 %all-to-all-start.4 = ((bf16[64,16,512]{2,1,0:T(8,128)(2,1)}), bf16[64,16,512]{2,1,0:T(8,128)(2,1)S(1)}, u32[]{:S(2)}, u32[]{:S(2)}) async-start(bf16[64,16,512]{2,1,0:T(8,128)(2,1)} %scatter_fusion), calls=%async_computation.4 | async-start | bytes 2097152 | tf_op jit(solution)/shard_map/all_to_all | solution.py:84
where the time goes:
time: 174 us; the launch traced here: 172 us
  waiting for transfers between devices  75.3 us (43%)
  local copies, waits for them, and re-layouts  51.2 us (29%)
  starting transfers between devices  32.6 us (19%)
  other arithmetic  12.2 us (7%)
    all_to_all x1, waiting for transfers between devices, per_device(): lax.all_to_all(out_weight, ('pipe', 'section'), split_axis=0, concat_axis...  13.7 us
    all_to_all x1, waiting for transfers between devices, per_device(): lax.all_to_all(held_state[1].astype(jnp.bfloat16), ('pipe', 'section'), s...  13.5 us
    unnamed x21, local copies, waits for them, and re-layouts  12.2 us
    all_to_all x1, waiting for transfers between devices, per_device(): lax.all_to_all(held_state[2].astype(jnp.bfloat16), ('pipe', 'section'), s...  11.8 us
    all_to_all x1, waiting for transfers between devices, per_device(): lax.all_to_all(held_state[0], ('pipe', 'section'), split_axis=1, concat_a...  11.7 us
    all_to_all x1, waiting for transfers between devices, per_device(): lax.all_to_all(out_one.astype(jnp.bfloat16), ('pipe', 'section'), split_a...  10.9 us
    all_to_all x1, waiting for transfers between devices, per_device(): lax.all_to_all(out_two.astype(jnp.bfloat16), ('pipe', 'section'), split_a...  10 us
    all_to_all x1, starting transfers between devices, per_device(): lax.all_to_all(held_state[1].astype(jnp.bfloat16), ('pipe', 'section'), s...  8.58 us
  transfers between devices with their start and end apart: 7, of which 7 were waited for; matrix products, arithmetic and copies ran while one was open for 27% of the time, Pallas kernels for 0%

commit v1 on v0

v1 whole, which is shorter than its diff:
```python
import functools

import jax
import jax.numpy as jnp
from jax import lax
from jax.experimental import pallas as pl
from jax.experimental.pallas import tpu as pltpu
from jax.sharding import PartitionSpec as P

LEARN_RATE = 0.01
BETA_ONE = 0.9
BETA_TWO = 0.95
EPSILON = 1e-08
DECAY_RATE = 0.1
MESH = pl.DeviceIdType.MESH
LAYERS = 12
BAND = 16
COLS = 512

def section_layers(section):
    last = section + min(section + 1, 4)
    return list(range(section + max(0, section - 4), last + 1))


CANDIDATES = [sorted(set(section_layers(x) + section_layers(x + 4))) for x in range(4)]
HELD = len(CANDIDATES[0])


def pick(index, values):
    out = jnp.int32(values[0])
    for at in range(1, len(values)):
        out = jnp.where(index == at, jnp.int32(values[at]), out)
    return out


def exchange_kernel(
    g_hbm, w_hbm, one_hbm, two_hbm, old_ref, new_ref, lost_ref, donor_ref,
    out_a, out_two, out_w,
    one_f, two_f, one_b, two_b,
    s1_w, s1_one, s1_two, s2s_w, s2s_one, s2s_two, s2r_w, s2r_one, s2r_two,
    g1, g2s, g2r, mean,
    r1s_a, r1s_two, r1s_w, r1r_a, r1r_two, r1r_w,
    r2s_a, v_a, v_two, v_w,
    t_pick, t_src, t_grad, t_lost, t_red, t_new, t_unit,
    send_sem, recv_sem, local_sem,
):
    pipe = lax.axis_index("pipe")
    section = lax.axis_index("section")
    tp = lax.axis_index("tp")
    y = (pipe // 2) * 2 + section // 4
    x = section % 4
    c = pipe % 2

    def device(yy, xx, cc):
        return ((yy // 2) * 2 + cc, (yy % 2) * 4 + xx, tp)

    counters = {"remote": 0, "local": 0}

    def remote(src, dst, target):
        at = counters["remote"]
        counters["remote"] = at + 1
        copy = pltpu.make_async_remote_copy(
            src_ref=src, dst_ref=dst, send_sem=send_sem.at[at], recv_sem=recv_sem.at[at],
            device_id=target, device_id_type=MESH,
        )
        copy.start()
        return copy

    def local(src, dst):
        at = counters["local"]
        counters["local"] = at + 1
        copy = pltpu.make_async_copy(src, dst, local_sem.at[at])
        copy.start()
        return copy

    def wait(copies):
        for copy in copies:
            copy.wait()

    x_core = [(dx, dc) for dx in (1, 3, 2) for dc in (0, 1)] + [(0, 1)]
    y_core = [(dy, dc) for dy in (1, 3, 2) for dc in (0, 1)] + [(0, 1)]

    load_one = local(one_hbm, one_f)
    load_two = local(two_hbm, two_f)

    barrier = pltpu.get_barrier_semaphore()
    greeted = [((y, (x + dx) % 4, (c + dc) % 2)) for dx, dc in x_core]
    greeted += [(((y + dy) % 4, x, (c + dc) % 2)) for dy, dc in y_core[:-1]]
    for yy, xx, cc in greeted:
        pl.semaphore_signal(barrier, inc=1, device_id=device(yy, xx, cc), device_id_type=MESH)
    pl.semaphore_wait(barrier, len(greeted))

    me_y = (y * 2 + c) * 2
    me_x = (x * 2 + c) * 2
    grad_one = []
    for dy, dc in y_core:
        yy, cc = (y + dy) % 4, (c + dc) % 2
        grad_one.append(remote(g_hbm.at[:, :, cc, yy], g1.at[pl.ds(me_y, 2)], device(yy, x, cc)))
    grad_one.append(local(g_hbm.at[:, :, c, y], g1.at[pl.ds(me_y, 2)]))

    def state_first(src, dst):
        copies = []
        for dx, dc in x_core:
            xx, cc = (x + dx) % 4, (c + dc) % 2
            copies.append(remote(src.at[:, xx * 2 + cc], dst.at[pl.ds(me_x, 2)], device(y, xx, cc)))
        copies.append(local(src.at[:, x * 2 + c], dst.at[pl.ds(me_x, 2)]))
        return copies

    first_w = state_first(w_hbm, s1_w)

    def narrow(src, dst):
        def body(at, carry):
            dst[at // 8, at % 8] = src[at // 8, at % 8].astype(jnp.bfloat16)
            return carry

        lax.fori_loop(0, 16, body, 0)

    load_one.wait()
    narrow(one_f, one_b)
    first_one = state_first(one_b, s1_one)
    load_two.wait()
    narrow(two_f, two_b)

    lost = lost_ref[0]
    lost_half, lost_core = lost // 2, lost % 2
    row = y % 2
    for j in range(8):
        layer = 4 * row + j
        donor = lost_ref[donor_ref[layer]]
        there = old_ref[donor, layer]
        twin = old_ref[donor, jnp.maximum(layer - 1, 0)]
        slot = jnp.where((layer > 0) & (twin == there), 1, 0)
        t_pick[j] = ((there % 4) * 2 + donor % 2) * 2 + slot
    for layer in range(LAYERS):
        donor = lost_ref[donor_ref[layer]]
        there = old_ref[donor, layer]
        t_src[layer] = ((donor // 2) * 2 + there // 4) * 8 + layer - 4 * (there // 4)
    for k in range(HELD):
        layer = pick(x, [CANDIDATES[at][k] for at in range(4)])
        for relay in range(4):
            there = old_ref[relay, layer]
            twin = old_ref[relay, jnp.maximum(layer - 1, 0)]
            slot = jnp.where((layer > 0) & (twin == there), 1, 0)
            held = (there % 4 == x) & (lost != relay)
            from_y = (relay // 2) * 2 + there // 4
            t_grad[k * 4 + relay] = jnp.where(held, (from_y * 2 + relay % 2) * 2 + slot, 16)
    for e in range(4):
        t_lost[e] = ((lost_half * 2 + e // 2) * 2 + lost_core) * 2 + e % 2
    new_at = [new_ref[layer] for layer in range(LAYERS)]
    inverse = [jnp.int32(0)] * 16
    for layer in range(LAYERS):
        there = new_at[layer]
        slot = jnp.int32(0)
        for before in range(layer):
            slot = slot + jnp.where(new_at[before] == there, 1, 0)
        t_red[layer] = (there % 4) * (HELD + 4) + HELD + (there // 4) * 2 + slot
        place = there * 2 + slot
        inverse = [jnp.where(place == at, layer, inverse[at]) for at in range(16)]
    for xx in range(4):
        for e in range(4):
            t_new[xx * 4 + e] = inverse[((e // 2) * 4 + xx) * 2 + e % 2]
    held_at = [pick(x, [CANDIDATES[at][k] for at in range(4)]) for k in range(HELD)]
    entries = {}
    for relay in range(4):
        for r in range(2):
            first = jnp.int32(0)
            for layer in range(LAYERS):
                first = first + jnp.where(old_ref[relay, layer] < r * 4 + x, 1, 0)
            for slot in range(2):
                position = jnp.int32(0)
                for k in range(HELD):
                    position = position + jnp.where(held_at[k] < first + slot, 1, 0)
                entries[relay, r, slot] = jnp.minimum(position, HELD - 1)
    for yy in range(4):
        half, r = yy // 2, yy % 2
        here = lost_half == half
        for slot in range(2):
            even, odd = entries[half * 2, r, slot], entries[half * 2 + 1, r, slot]
            t_unit[yy * 4 + slot] = jnp.where(here & (lost_core == 0), odd, even)
            t_unit[yy * 4 + 2 + slot] = jnp.where(here, HELD + r * 2 + slot, odd)

    g1[16] = jnp.zeros((4, BAND, COLS), jnp.bfloat16)
    wait(grad_one)

    def grad_merge(k, carry):
        total = g1[t_grad[k * 4]].astype(jnp.float32)
        for relay in range(1, 4):
            total = total + g1[t_grad[k * 4 + relay]].astype(jnp.float32)
        g2s[:, k] = total.astype(jnp.bfloat16)
        return carry

    lax.fori_loop(0, HELD, grad_merge, 0)

    def grad_lost(e, carry):
        g2s[:, HELD + e] = g1[t_lost[e]]
        return carry

    lax.fori_loop(0, 4, grad_lost, 0)

    def x_exchange(src, dst):
        copies = []
        for dx in (1, 3, 2):
            xx = (x + dx) % 4
            copies.append(remote(src.at[xx], dst.at[x], device(y, xx, c)))
        copies.append(local(src.at[x], dst.at[x]))
        return copies

    def y_exchange(src, dst):
        copies = []
        for dy in (1, 3, 2):
            yy = (y + dy) % 4
            copies.append(remote(src.at[yy], dst.at[y], device(yy, x, c)))
        copies.append(local(src.at[y], dst.at[y]))
        return copies

    grad_two = x_exchange(g2s, g2r)

    def state_second(src, send, dst):
        def body(j, carry):
            send[:, j] = src[t_pick[j]]
            return carry

        lax.fori_loop(0, 8, body, 0)
        return y_exchange(send, dst)

    wait(first_w)
    second_w = state_second(s1_w, s2s_w, s2r_w)

    def state_at(ref, layer):
        at = t_src[layer]
        return ref[at // 8, at % 8]

    wait(second_w)

    def pack_w(i, carry):
        r1s_w[i // 4, i % 4] = state_at(s2r_w, t_new[i])
        return carry

    lax.fori_loop(0, 16, pack_w, 0)
    back_w = x_exchange(r1s_w, r1r_w)
    first_two = state_first(two_b, s1_two)

    wait(first_one)
    second_one = state_second(s1_one, s2s_one, s2r_one)

    wait(grad_two)
    for layer in range(LAYERS):
        at = t_red[layer]
        total = g2r[at // (HELD + 4), at % (HELD + 4)].astype(jnp.float32)
        for xx in range(4):
            if layer in CANDIDATES[xx]:
                total = total + g2r[xx, CANDIDATES[xx].index(layer)].astype(jnp.float32)
        mean[layer] = total * 0.25
    for xx in range(4):
        for k in range(HELD):
            r1s_a[xx, k] = mean[CANDIDATES[xx][k]].astype(jnp.bfloat16)

    wait(second_one)

    def pack_one(i, carry):
        layer = t_new[i]
        value = BETA_ONE * state_at(s2r_one, layer).astype(jnp.float32) + (1.0 - BETA_ONE) * mean[layer]
        r1s_a[i // 4, HELD + i % 4] = value.astype(jnp.bfloat16)
        return carry

    lax.fori_loop(0, 16, pack_one, 0)
    back_a = x_exchange(r1s_a, r1r_a)

    def y_return(src_of, dst):
        copies = []
        for dy in (1, 3, 2):
            yy = (y + dy) % 4
            copies.append(remote(src_of(yy), dst.at[:, y], device(yy, x, c)))
        copies.append(local(src_of(y), dst.at[:, y]))
        return copies

    wait(back_w)
    down_w = y_return(lambda yy: r1r_w.at[:, pl.ds((yy % 2) * 2, 2)], v_w)

    wait(first_two)
    second_two = state_second(s1_two, s2s_two, s2r_two)

    wait(back_a)

    def pack_units(i, carry):
        r2s_a[i // 4, :, i % 4] = r1r_a[:, t_unit[i]]
        return carry

    lax.fori_loop(0, 16, pack_units, 0)
    down_a = y_return(lambda yy: r2s_a.at[yy], v_a)

    wait(second_two)

    def pack_two(i, carry):
        layer = t_new[i]
        grad = mean[layer]
        value = BETA_TWO * state_at(s2r_two, layer).astype(jnp.float32) + (1.0 - BETA_TWO) * grad * grad
        r1s_two[i // 4, i % 4] = value.astype(jnp.bfloat16)
        return carry

    lax.fori_loop(0, 16, pack_two, 0)
    back_two = x_exchange(r1s_two, r1r_two)

    def core_swap(src, dst):
        return [remote(src, dst.at[:, c], device(y, x, 1 - c)), local(src, dst.at[:, c])]

    wait(down_w)
    swaps = core_swap(v_w, out_w)
    wait(back_two)
    down_two = y_return(lambda yy: r1r_two.at[:, pl.ds((yy % 2) * 2, 2)], v_two)
    wait(down_a)
    swaps += core_swap(v_a, out_a)
    wait(down_two)
    swaps += core_swap(v_two, out_two)
    wait(swaps)


def exchange(grads, weights, one, two, old_section, new_section, lost_pipe, donor_offset):
    bf16, f32, i32 = jnp.bfloat16, jnp.float32, jnp.int32
    any_space = pl.BlockSpec(memory_space=pl.ANY)
    smem = pl.BlockSpec(memory_space=pltpu.SMEM)
    vm = lambda shape, dtype=bf16: pltpu.VMEM(shape + (BAND, COLS), dtype)
    state = (2, 8, 4)
    return pl.pallas_call(
        exchange_kernel,
        out_shape=(
            jax.ShapeDtypeStruct((4, 2, 4, 4, BAND, COLS), bf16),
            jax.ShapeDtypeStruct((4, 2, 4, 2, BAND, COLS), bf16),
            jax.ShapeDtypeStruct((4, 2, 4, 2, BAND, COLS), bf16),
        ),
        in_specs=[any_space] * 4 + [smem] * 4,
        out_specs=(any_space, any_space, any_space),
        scratch_shapes=[
            vm(state, f32), vm(state, f32), vm(state), vm(state),
            vm((16, 4)), vm((16, 4)), vm((16, 4)),
            vm((4, 8)), vm((4, 8)), vm((4, 8)),
            vm((4, 8)), vm((4, 8)), vm((4, 8)),
            vm((17, 4)), vm((4, HELD + 4)), vm((4, HELD + 4)), vm((LAYERS,), f32),
            vm((4, HELD + 4)), vm((4, 4)), vm((4, 4)),
            vm((4, HELD + 4)), vm((4, 4)), vm((4, 4)),
            vm((4, 4, 4)), vm((4, 4, 4)), vm((4, 4, 2)), vm((4, 4, 2)),
            pltpu.SMEM((8,), i32), pltpu.SMEM((LAYERS,), i32), pltpu.SMEM((HELD * 4,), i32), pltpu.SMEM((4,), i32),
            pltpu.SMEM((LAYERS,), i32), pltpu.SMEM((16,), i32), pltpu.SMEM((16,), i32),
            pltpu.SemaphoreType.DMA((64,)), pltpu.SemaphoreType.DMA((64,)), pltpu.SemaphoreType.DMA((32,)),
        ],
        compiler_params=pltpu.CompilerParams(collective_id=0, has_side_effects=True, vmem_limit_bytes=48 << 20),
        name="exchange",
    )(
        grads.reshape(2, 4, 2, 4, BAND, COLS),
        weights.reshape(2, 8, 4, BAND, COLS),
        one.reshape(2, 8, 4, BAND, COLS),
        two.reshape(2, 8, 4, BAND, COLS),
        old_section, new_section, lost_pipe, donor_offset,
    )


def adam_kernel(info, a_ref, two_in, w_in, w_ref, one_ref, two_ref, out_w, out_one, out_two):
    slot = pl.program_id(0)
    rows = out_w.shape[1]
    keep = slot < info[2]

    def finish(weight, next_one, next_two):
        update = next_one / (jnp.sqrt(next_two) + EPSILON) + DECAY_RATE * weight
        next_weight = weight - LEARN_RATE * update
        out_w[0] = jnp.where(keep, next_weight, 0.0).astype(jnp.bfloat16)
        out_one[0] = jnp.where(keep, next_one, 0.0)
        out_two[0] = jnp.where(keep, next_two, 0.0)

    def wide(ref):
        return ref[...].astype(jnp.float32).reshape(rows, COLS)

    @pl.when(info[0] == 1)
    def _():
        finish(wide(w_in), wide(a_ref), wide(two_in))

    @pl.when(info[0] == 0)
    def _():
        grad = wide(a_ref)
        next_one = BETA_ONE * one_ref[0] + (1.0 - BETA_ONE) * grad
        next_two = BETA_TWO * two_ref[0] + (1.0 - BETA_TWO) * grad * grad
        finish(w_ref[0].astype(jnp.float32), next_one, next_two)


def adam(info, units, lost_two, lost_w, weights, one, two):
    chunk = 128
    moved = lambda at: pl.BlockSpec((1, 2, 4, 1, BAND, COLS), at)
    own = pl.BlockSpec(
        (1, chunk, COLS), lambda s, i, info: (jnp.where(info[0] == 1, 0, s), jnp.where(info[0] == 1, 0, i), 0)
    )
    lost_only = moved(
        lambda s, i, info: (jnp.where(info[0] == 1, i, 0), 0, 0, jnp.where(info[0] == 1, s, 0), 0, 0)
    )
    out = pl.BlockSpec((1, chunk, COLS), lambda s, i, info: (s, i, 0))
    return pl.pallas_call(
        adam_kernel,
        out_shape=(
            jax.ShapeDtypeStruct(weights.shape, jnp.bfloat16),
            jax.ShapeDtypeStruct(one.shape, jnp.float32),
            jax.ShapeDtypeStruct(two.shape, jnp.float32),
        ),
        grid_spec=pltpu.PrefetchScalarGridSpec(
            num_scalar_prefetch=1,
            grid=(2, 4),
            in_specs=[
                moved(lambda s, i, info: (i, 0, 0, info[1] + s, 0, 0)),
                lost_only, lost_only, own, own, own,
            ],
            out_specs=(out, out, out),
        ),
        compiler_params=pltpu.CompilerParams(dimension_semantics=("arbitrary", "arbitrary")),
        name="adam",
    )(info, units, lost_two, lost_w, weights, one, two)


def per_device(weights, first_moment, second_moment, gradients, old_section, new_section, lost_pipe, donor_offset):
    pipe, section = lax.axis_index("pipe"), lax.axis_index("section")
    weights, one, two, grads = weights[0, 0], first_moment[0, 0], second_moment[0, 0], gradients[0, 0]
    lost = lost_pipe[0]
    is_lost = lost == pipe
    own_map = jnp.where(is_lost, new_section, jnp.sum(jnp.where(jnp.arange(4)[:, None] == pipe, old_section, 0), axis=0))
    count = jnp.sum((own_map == section).astype(jnp.int32))
    base = jnp.where(is_lost, 2, jnp.where(lost // 2 == pipe // 2, 0, (pipe % 2) * 2))
    info = jnp.stack([is_lost.astype(jnp.int32), base.astype(jnp.int32), count])
    units, lost_two, lost_w = exchange(grads, weights, one, two, old_section, new_section, lost_pipe, donor_offset)
    out_w, out_one, out_two = adam(info, units, lost_two, lost_w, weights, one, two)
    return out_w[None, None], out_one[None, None], out_two[None, None]


def solution(mesh):
    big, small = P("pipe", "section", None, "tp", None), P()
    return jax.shard_map(
        per_device,
        mesh=mesh,
        in_specs=(big, big, big, big, small, small, small, small),
        out_specs=(big, big, big),
        check_vma=False,
    )
```

time: 174 us -> 106 us (0.61)
  Pallas kernels: 0 us -> 90.8 us
  waiting for transfers between devices: 75.3 us -> 0 us
  local copies, waits for them, and re-layouts: 51.2 us -> 7.06 us
  starting transfers between devices: 32.6 us -> 0 us
  other arithmetic: 12.2 us -> 3.37 us
  between operations: 0.92 us -> 3.94 us
    pallas_call x0 -> x2, Pallas kernels: none -> 90.8 us  [the longest x1 82.5 us: exchange(): pl.pallas_call(exchange_kernel, out_shape=(jax.ShapeDtypeStruct((4, 2, 4,...]
    all_to_all x7 -> x0, waiting for transfers between devices: 75.3 us -> none  [the longest x1 13.7 us: per_device(): lax.all_to_all(out_weight, ('pipe', 'section'), split_axis=0, concat_axis...]
    all_to_all x7 -> x0, starting transfers between devices: 32.6 us -> none  [the longest x1 8.58 us: per_device(): lax.all_to_all(held_state[1].astype(jnp.bfloat16), ('pipe', 'section'), s...]
    scatter x3 -> x0, local copies, waits for them, and re-layouts: 16.4 us -> none  [the longest x1 6.25 us: per_device(): jnp.zeros(piece_weight.shape, jnp.bfloat16).at[place_index].set(next_weight)]
    gather x9 -> x0, local copies, waits for them, and re-layouts: 10.2 us -> none  [the longest x1 2.75 us: per_device(): weight_now = piece_weight[source_index].astype(jnp.float32)]
    convert_element_type x9 -> x0, other arithmetic: 9.35 us -> none  [the longest x1 2.54 us: per_device(): next_weight = (weight_now - LEARN_RATE * update).astype(jnp.bfloat16)]
    all_to_all x7 -> x0, local copies, waits for them, and re-layouts: 5.32 us -> none  [the longest x2 2.46 us: per_device(): lax.all_to_all(held_state[0], ('pipe', 'section'), split_axis=1, concat_a...]
    unnamed x21 -> x16, local copies, waits for them, and re-layouts: 12.2 us -> 7.06 us
  transfers between devices with their start and end apart: 7 -> 0, of which waited for: 7 -> 0; matrix products, arithmetic and copies ran while one was open for 27% -> 0% of each run, Pallas kernels for 0% -> 0%
where the time goes in v1:
time: 106 us; the launch traced here: 105 us
  Pallas kernels  90.8 us (86%)
  local copies, waits for them, and re-layouts  7.06 us (7%)
  between operations  3.94 us (4%)
  other arithmetic  3.37 us (3%)
    pallas_call x1, Pallas kernels, exchange(): pl.pallas_call(exchange_kernel, out_shape=(jax.ShapeDtypeStruct((4, 2, 4,...  82.5 us
    pallas_call x1, Pallas kernels, adam(): pl.pallas_call(adam_kernel, out_shape=(jax.ShapeDtypeStruct(weights.shape...  8.28 us
    unnamed x16, local copies, waits for them, and re-layouts  7.06 us

profile of v1, /device:TPU:1, one launch (start us, length us, event | category | flops | bytes accessed | tf_op | source)
XLA Modules:
  0.0 105.2 jit_solution(9683443432483824234)
XLA Ops:
  3.9 0.8 select_reduce_fusion
  4.7 1.3 %fusion = s32[]{:T(128)} fusion(s32[12]{0:T(128)} %new_ref.1, s32[12]{0:T(128)S(1)} %select_reduce_fusion, pred[]{:T(512)S(6)} %eq.25, s32[]{:T(128)S(6)} %axis_index.28), kind=kLoop, calls=%fused_computation.3 | loop fusion | flops 47 | bytes 105 | tf_op jit(solution)/shard_map/reduce_sum | solution.py:421
  6.0 1.3 %pad_add_fusion.info = s32[3]{0:T(128)} fusion(s32[1]{0:T(128)} %bitcast.3, s32[1]{0:T(128)} %bitcast.2, s32[1]{0:T(128)} %bitcast.1), kind=kLoop, calls=%fused_computation.4 | loop fusion | flops 6 | bytes 24 | tf_op jit(solution)/shard_map/stack | solution.py:423
  7.3 0.0 copy-start
  7.3 1.2 %copy-done = bf16[1,1,2,512,512]{4,3,2,1,0:T(8,128)(2,1)S(1)} copy-done((bf16[1,1,2,512,512]{4,3,2,1,0:T(8,128)(2,1)S(1)}, bf16[1,1,2,512,512]{4,3,2,1,0:T(8,128)(2,1)}, u32[]{:S(2)}) %copy-start) | copy-done | bytes 1048600
  8.5 0.0 copy-start.1
  8.5 1.2 %copy-done.1 = bf16[1,1,2,512,512]{4,3,2,1,0:T(8,128)(2,1)S(1)} copy-done((bf16[1,1,2,512,512]{4,3,2,1,0:T(8,128)(2,1)S(1)}, bf16[1,1,2,512,512]{4,3,2,1,0:T(8,128)(2,1)}, u32[]{:S(2)}) %copy-start.1) | copy-done | bytes 1048600
  9.7 0.0 copy-start.4
  9.7 0.7 copy-done.4
  10.4 0.0 copy-start.5
  10.4 0.7 copy-done.5
  11.1 0.0 copy-start.6
  11.1 0.7 copy-done.6
  11.7 0.0 copy-start.7
  11.7 0.7 copy-done.7
  12.4 82.5 %exchange.1 = (bf16[4,2,4,4,16,512]{5,4,3,2,1,0:T(8,128)(2,1)}, bf16[4,2,4,2,16,512]{5,4,3,2,1,0:T(8,128)(2,1)S(1)}, bf16[4,2,4,2,16,512]{5,4,3,2,1,0:T(8,128)(2,1)S(1)}) custom-call(bf16[2,4,2,4,16,512]{5,4,3,2,1,0:T(8,128)(2,1)S(1)} %bitcast.17, bf16[2,8,4,16,512]{4,3,2,1,0:T(8,128)(2,1)S(1)} %bitcast.16, f32[2,8,4,16,512]{4,3,2,1,0:T(8,128)} %bitcast.23, ...), custom_call_target="tpu_custom_call" | custom-call | tf_op jit(solution)/shard_map/exchange/pallas_call | solution.py:324
  94.9 0.0 copy-start.2
  94.9 1.0 copy-done.2
  95.9 0.0 copy-start.3
  95.9 1.0 copy-done.3
  96.9 8.3 %adam.1 = (bf16[2,512,512]{2,1,0:T(8,128)(2,1)}, f32[2,512,512]{2,1,0:T(8,128)}, f32[2,512,512]{2,1,0:T(8,128)}) custom-call(s32[3]{0:T(128)} %pad_add_fusion.info, bf16[4,2,4,4,16,512]{5,4,3,2,1,0:T(8,128)(2,1)} %get-tuple-element.9.a_ref, bf16[4,2,4,2,16,512]{5,4,3,2,1,0:T(8,128)(2,1)} %copy-done.2, bf16[4,2,4,2,16,512]{5,4,3,2,1,0:T(8,128)(2,1)} %copy-done.3, ...), custom_call_target="tpu_custom_call" | custom-call | tf_op jit(solution)/shard_map/adam/pallas_call | solution.py:394
  (1 shorter events, 0.0 us)
Async XLA Ops:
  7.3 1.2 %copy-start = (bf16[1,1,2,512,512]{4,3,2,1,0:T(8,128)(2,1)S(1)}, bf16[1,1,2,512,512]{4,3,2,1,0:T(8,128)(2,1)}, u32[]{:S(2)}) copy-start(bf16[1,1,2,512,512]{4,3,2,1,0:T(8,128)(2,1)} %param.8) | copy-start | bytes 3145732
  8.5 1.2 %copy-start.1 = (bf16[1,1,2,512,512]{4,3,2,1,0:T(8,128)(2,1)S(1)}, bf16[1,1,2,512,512]{4,3,2,1,0:T(8,128)(2,1)}, u32[]{:S(2)}) copy-start(bf16[1,1,2,512,512]{4,3,2,1,0:T(8,128)(2,1)} %param.11) | copy-start | bytes 3145732
  9.7 0.7 copy-start.4
  10.4 0.7 copy-start.5
  11.1 0.7 copy-start.6
  11.7 0.7 copy-start.7
  94.9 1.0 copy-start.2
  95.9 1.0 copy-start.3

commit v2 on v0

v2 whole, which is shorter than its diff:
```python
from typing import Any, NamedTuple

import jax
import jax.numpy as jnp
from jax import lax
from jax.experimental import pallas as pl
from jax.experimental.pallas import tpu as pltpu
from jax.sharding import PartitionSpec as P

LEARN_RATE = 0.01
BETA_ONE = 0.9
BETA_TWO = 0.95
EPSILON = 1e-08
DECAY_RATE = 0.1
MESH = pl.DeviceIdType.MESH
LAYERS = 12
BAND = 16
COLS = 512

WEIGHT, FIRST, SECOND = range(3)
ALONG_X, ALONG_Y = range(2)
STREAMS = (
    (WEIGHT, ALONG_X, 0, 256),
    (WEIGHT, ALONG_X, 256, 256),
    (FIRST, ALONG_X, 0, 512),
    (SECOND, ALONG_Y, 0, 384),
    (SECOND, ALONG_Y, 384, 128),
)
W0, W1, ONE, TWO0, TWO1 = range(5)
S1, S2, R1, R2, R3, LOAD = range(6)
GRADS, MEANS, SMALL = range(10, 13)


def section_layers(section):
    last = section + min(section + 1, 4)
    return list(range(section + max(0, section - 4), last + 1))


CANDIDATES = [sorted(set(section_layers(x) + section_layers(x + 4))) for x in range(4)]
HELD = len(CANDIDATES[0])


class Buffers(NamedTuple):
    grads_in: Any
    state_in: Any
    maps_in: Any
    final: Any
    narrow: Any
    grad_one: Any
    grad_send: Any
    grad_two: Any
    mean: Any
    mean_send: Any
    mean_back: Any
    mean_down: Any
    pair_down: Any
    half_mean: Any
    half: Any
    units: Any
    lost_two: Any
    lost_w: Any
    one: Any
    two_send: Any
    two: Any
    back_send: Any
    back: Any
    maps: Any
    pick: Any
    src: Any
    grad_at: Any
    lost_at: Any
    sum_at: Any
    new_at: Any
    new_has: Any
    mean_at: Any
    unit_at: Any
    flags: Any
    sent: Any
    got: Any


def pick(index, values):
    out = jnp.int32(values[0])
    for at in range(1, len(values)):
        out = jnp.where(index == at, jnp.int32(values[at]), out)
    return out


def update(weight, next_one, next_two):
    change = next_one / (jnp.sqrt(next_two) + EPSILON) + DECAY_RATE * weight
    return weight - LEARN_RATE * change


def exchange_kernel(tree, *refs):
    ref = jax.tree.unflatten(tree, refs)
    pipe, section, tp = lax.axis_index("pipe"), lax.axis_index("section"), lax.axis_index("tp")
    y = (pipe // 2) * 2 + section // 4
    x = section % 4
    c = pipe % 2
    ring = (1, 3, 2)
    with_core = [(step, dc) for step in ring for dc in (0, 1)] + [(0, 1)]
    pending = {}

    def device(yy, xx, cc):
        return ((yy // 2) * 2 + cc, (yy % 2) * 4 + xx, tp)

    def begin(key, sends, own, landed, left):
        at = len(pending)
        assert at < ref.sent.shape[0]
        for src, dst, target in sends:
            pltpu.make_async_remote_copy(
                src_ref=src, dst_ref=dst, send_sem=ref.sent.at[at], recv_sem=ref.got.at[at],
                device_id=target, device_id_type=MESH,
            ).start()
        for src, dst in own:
            pltpu.make_async_copy(src, dst, ref.got.at[at]).start()
        pending[key] = (at, landed, left)

    done = set()

    def need(*keys):
        for key in keys:
            if key in done:
                continue
            done.add(key)
            at, landed, left = pending[key]
            for part in landed:
                pltpu.make_async_copy(part, part, ref.got.at[at]).wait()
            for part in left:
                pltpu.make_async_copy(part, part, ref.sent.at[at]).wait()

    barrier = pltpu.get_barrier_semaphore()
    greeted = [(y, (x + dx) % 4, (c + dc) % 2) for dx, dc in with_core]
    greeted += [((y + dy) % 4, x, (c + dc) % 2) for dy, dc in with_core[:-1]]
    for yy, xx, cc in greeted:
        pl.semaphore_signal(barrier, inc=1, device_id=device(yy, xx, cc), device_id_type=MESH)
    for array in (FIRST, SECOND, WEIGHT):
        begin((LOAD, array), (), [(ref.state_in[array], ref.final[array])], [ref.final[array]], ())
    for k in range(4):
        begin((LOAD, SMALL + k), (), [(ref.maps_in[k], ref.maps[k])], [ref.maps[k]], ())
    pl.semaphore_wait(barrier, len(greeted))

    def first(key, axis, src, dst):
        me = pl.ds(((x if axis == ALONG_X else y) * 2 + c) * 2, 2)
        sends = []
        for step, dc in with_core:
            cc = (c + dc) % 2
            if axis == ALONG_X:
                xx = (x + step) % 4
                sends.append((src.at[:, xx, cc], dst.at[me], device(y, xx, cc)))
            else:
                yy = (y + step) % 4
                sends.append((src.at[:, :, cc, yy], dst.at[me], device(yy, x, cc)))
        own = src.at[:, x, c] if axis == ALONG_X else src.at[:, :, c, y]
        begin(key, sends, [(own, dst.at[me])], [dst.at[pl.ds(0, 16)]], [dst.at[pl.ds(0, 14)]])

    def along(key, axis, src_of, dst):
        if axis == ALONG_X:
            sends = [(src_of((x + d) % 4), dst.at[x], device(y, (x + d) % 4, c)) for d in ring]
            own = [(src_of(x), dst.at[x])]
        else:
            sends = [(src_of((y + d) % 4), dst.at[y], device((y + d) % 4, x, c)) for d in ring]
            own = [(src_of(y), dst.at[y])]
        begin(key, sends, own, [dst], [dst.at[pl.ds(0, 3)]])

    def down(key, src_of, dst):
        sends = [(src_of((y + d) % 4), dst.at[:, y], device((y + d) % 4, x, c)) for d in ring]
        begin(key, sends, [(src_of(y), dst.at[:, y])], [dst], [dst.at[:, pl.ds(0, 3)]])

    def columns(stream, source):
        _, _, start, width = STREAMS[stream]
        return source if width == COLS else source.at[..., pl.ds(start, width)]

    def narrow(array):
        wide, thin = ref.final[array], ref.narrow[array - 1]
        need((LOAD, array))

        def body(at, carry):
            thin[at // 8, (at // 2) % 4, at % 2] = wide[at // 8, (at // 2) % 4, at % 2].astype(jnp.bfloat16)
            return carry

        lax.fori_loop(0, 16, body, 0)

    def state_first(stream):
        array, axis, _, _ = STREAMS[stream]
        source = ref.state_in[array] if array == WEIGHT else ref.narrow[array - 1]
        first((S1, stream), axis, columns(stream, source), ref.one[stream])

    def tables():
        need(*[(LOAD, SMALL + k) for k in range(4)])
        old, new, lost_ref, donor_ref = ref.maps
        lost = lost_ref[0]
        lost_half, lost_core = lost // 2, lost % 2

        def placed(relay, layer):
            there = old[relay, layer]
            twin = old[relay, jnp.maximum(layer - 1, 0)]
            return there, jnp.where((layer > 0) & (twin == there), 1, 0)

        held_at = [pick(x, [CANDIDATES[at][k] for at in range(4)]) for k in range(HELD)]
        for j in range(8):
            layer = 4 * (y % 2) + j
            donor = lost_ref[donor_ref[layer]]
            there, slot = placed(donor, layer)
            ref.pick[ALONG_X][j] = ((there % 4) * 2 + donor % 2) * 2 + slot
        for k in range(HELD):
            donor = lost_ref[donor_ref[held_at[k]]]
            there, slot = placed(donor, held_at[k])
            ref.pick[ALONG_Y][k] = (((donor // 2) * 2 + there // 4) * 2 + donor % 2) * 2 + slot
        for layer in range(LAYERS):
            donor = lost_ref[donor_ref[layer]]
            there = old[donor, layer]
            ref.src[ALONG_X][layer] = ((donor // 2) * 2 + there // 4) * 8 + layer - 4 * (there // 4)
            spots = [at * HELD + (CANDIDATES[at].index(layer) if layer in CANDIDATES[at] else 0) for at in range(4)]
            ref.src[ALONG_Y][layer] = pick(there % 4, spots)
        for k in range(HELD):
            for relay in range(4):
                there, slot = placed(relay, held_at[k])
                held = (there % 4 == x) & (lost != relay)
                from_y = (relay // 2) * 2 + there // 4
                ref.grad_at[k * 4 + relay] = jnp.where(held, (from_y * 2 + relay % 2) * 2 + slot, 16)
        for e in range(4):
            ref.lost_at[e] = ((lost_half * 2 + e // 2) * 2 + lost_core) * 2 + e % 2
        new_at = [new[layer] for layer in range(LAYERS)]
        inverse = [jnp.int32(LAYERS)] * 16
        for layer in range(LAYERS):
            there = new_at[layer]
            slot = jnp.int32(0)
            for before in range(layer):
                slot = slot + jnp.where(new_at[before] == there, 1, 0)
            ref.sum_at[layer] = (there % 4) * (HELD + 4) + HELD + (there // 4) * 2 + slot
            place = there * 2 + slot
            inverse = [jnp.where(place == at, layer, inverse[at]) for at in range(16)]
        for xx in range(4):
            for e in range(4):
                layer = inverse[((e // 2) * 4 + xx) * 2 + e % 2]
                ref.new_at[xx * 4 + e] = jnp.minimum(layer, LAYERS - 1)
                ref.new_has[xx * 4 + e] = jnp.where(layer < LAYERS, 1, 0)
        entries = {}
        for relay in range(4):
            for r in range(2):
                start = jnp.int32(0)
                for layer in range(LAYERS):
                    start = start + jnp.where(old[relay, layer] < r * 4 + x, 1, 0)
                for slot in range(2):
                    position = jnp.int32(0)
                    for k in range(HELD):
                        position = position + jnp.where(held_at[k] < start + slot, 1, 0)
                    entries[relay, r, slot] = jnp.minimum(position, HELD - 1)
        for yy in range(4):
            half, r = yy // 2, yy % 2
            here = lost_half == half
            for slot in range(2):
                even, odd = entries[half * 2, r, slot], entries[half * 2 + 1, r, slot]
                ref.mean_at[yy * 2 + slot] = jnp.where(here & (lost_core == 0), odd, even)
                ref.unit_at[yy * 2 + slot] = jnp.where(here, HELD + r * 2 + slot, odd)
        is_lost = lost == pipe
        count = jnp.int32(0)
        for layer in range(LAYERS):
            count = count + jnp.where(old[pipe, layer] == section, 1, 0)
        ref.flags[0] = jnp.where(is_lost, 1, 0)
        ref.flags[1] = jnp.where(is_lost | ((lost_half != pipe // 2) & (c == 1)), 1, 0)
        ref.flags[2] = jnp.where(is_lost | (count > 1), 1, 0)

    def grad_second():
        held, send = ref.grad_one, ref.grad_send
        held[16] = jnp.zeros((4, BAND, COLS), jnp.bfloat16)
        need((S1, GRADS))

        def merge(k, carry):
            total = held[ref.grad_at[k * 4]].astype(jnp.float32)
            for relay in range(1, 4):
                total = total + held[ref.grad_at[k * 4 + relay]].astype(jnp.float32)
            send[:, k] = total.astype(jnp.bfloat16)
            return carry

        lax.fori_loop(0, HELD, merge, 0)

        def keep(e, carry):
            send[:, HELD + e] = held[ref.lost_at[e]]
            return carry

        lax.fori_loop(0, 4, keep, 0)
        along((S2, GRADS), ALONG_X, lambda xx: send.at[xx], ref.grad_two)

    def means_back():
        got, mean, send = ref.grad_two, ref.mean, ref.mean_send
        need((S2, GRADS))
        for layer in range(LAYERS):
            at = ref.sum_at[layer]
            total = got[at // (HELD + 4), at % (HELD + 4)].astype(jnp.float32)
            for xx in range(4):
                if layer in CANDIDATES[xx]:
                    total = total + got[xx, CANDIDATES[xx].index(layer)].astype(jnp.float32)
            mean[layer] = total * 0.25
        for xx in range(4):
            for k in range(HELD):
                send[xx, k] = mean[CANDIDATES[xx][k]].astype(jnp.bfloat16)
        along((R1, MEANS), ALONG_X, lambda xx: send.at[xx], ref.mean_back)

    def state_second(stream):
        axis = STREAMS[stream][1]
        src, send, table = ref.one[stream], ref.two_send[stream], ref.pick[axis]
        need((S1, stream))

        def body(j, carry):
            send[:, j] = src[table[j]]
            return carry

        lax.fori_loop(0, send.shape[1], body, 0)
        along((S2, stream), 1 - axis, lambda at: send.at[at], ref.two[stream])

    def state_back(stream):
        array, axis, start, width = STREAMS[stream]
        src, send, mean = ref.two[stream], ref.back_send[stream], ref.mean
        held = src.shape[1]
        need((S2, stream))

        def body(i, carry):
            layer = ref.new_at[i]
            at = ref.src[axis][layer]
            value = src[at // held, at % held].astype(jnp.float32)
            grad = mean[layer] if width == COLS else mean[layer, :, start : start + width]
            if array == FIRST:
                value = BETA_ONE * value + (1.0 - BETA_ONE) * grad
            elif array == SECOND:
                value = BETA_TWO * value + (1.0 - BETA_TWO) * grad * grad
            send[i // 4, i % 4] = jnp.where(ref.new_has[i] == 1, value, 0.0).astype(jnp.bfloat16)
            return carry

        lax.fori_loop(0, 16, body, 0)
        along((R1, stream), ALONG_X, lambda xx: send.at[xx], ref.back[stream])

    def means_down():
        send, got = ref.mean_down, ref.mean_back
        need((R1, MEANS))
        for i in range(8):
            send[i // 2, :, i % 2] = got[:, ref.mean_at[i]]
        down((R2, MEANS), lambda yy: send.at[yy], ref.half_mean)

    def state_down(stream):
        array = STREAMS[stream][0]
        got, dst = ref.back[stream], columns(stream, ref.half[array])
        need((R1, stream))
        if array != FIRST:
            down((R2, stream), lambda yy: got.at[:, pl.ds((yy % 2) * 2, 2)], dst)
            return
        send, means = ref.pair_down, ref.mean_back
        for i in range(8):
            at = ref.unit_at[i]
            layer = means[:, jnp.minimum(at, HELD - 1)]
            send[i // 2, :, i % 2] = jnp.where(at < HELD, layer, got[:, jnp.maximum(at - HELD, 0)])
        down((R2, stream), lambda yy: send.at[yy], dst)

    def swap(key, src, dst):
        begin(key, [(src, dst.at[:, c], device(y, x, 1 - c))], [(src, dst.at[:, c])], [dst], [src])

    def swap_units(key, unit, src):
        need((R2, key))
        swap((R3, key), src, ref.units.at[unit])

    def survivors(slot):
        need((R3, MEANS), (R3, ONE), (LOAD, WEIGHT))
        w, one, two = ref.final
        lost, unit, second = ref.flags[0] == 1, ref.flags[1], ref.flags[2] == 1

        def body(i, carry):
            xb, cb, yb = i // 8, (i // 4) % 2, i % 4
            grad = ref.units[unit, xb, cb, yb, slot].astype(jnp.float32)
            next_one = BETA_ONE * one[slot, xb, cb, yb] + (1.0 - BETA_ONE) * grad
            next_two = BETA_TWO * two[slot, xb, cb, yb] + (1.0 - BETA_TWO) * grad * grad
            next_w = update(w[slot, xb, cb, yb].astype(jnp.float32), next_one, next_two)
            next_one = jnp.where(lost, grad, next_one)
            if slot == 1:
                next_one, next_two, next_w = [jnp.where(second, v, 0.0) for v in (next_one, next_two, next_w)]
            one[slot, xb, cb, yb] = next_one
            two[slot, xb, cb, yb] = next_two
            w[slot, xb, cb, yb] = next_w.astype(jnp.bfloat16)
            return carry

        lax.fori_loop(0, 32, body, 0, unroll=2)

    def lost_weights(stream):
        need((R2, W0), (R2, W1), (R2, ONE), (R2, stream))
        start, width = STREAMS[stream][2:]
        w, one, two = ref.half

        def body(i, carry):
            at = (i // 4, i % 4, slice(None), slice(None), slice(start, start + width))
            weight, next_one, next_two = [v[at].astype(jnp.float32) for v in (w, one, two)]
            w[at] = update(weight, next_one, next_two).astype(jnp.bfloat16)
            return carry

        lax.fori_loop(0, 16, body, 0)
        swap((R3, stream, SECOND), columns(stream, two), columns(stream, ref.lost_two))
        swap((R3, stream, WEIGHT), columns(stream, w), columns(stream, ref.lost_w))

    def lost_state(stream):
        need((R3, stream, SECOND), (R3, stream, WEIGHT))
        start, width = STREAMS[stream][2:]
        w, _, two = ref.final
        lost = ref.flags[0] == 1
        cols = slice(start, start + width)

        def body(i, carry):
            slot, xb, cb = i // 8, (i // 2) % 4, i % 2
            to, come = (slot, xb, cb, slice(None), slice(None), cols), (xb, cb, slice(None), slot, slice(None), cols)
            two[to] = jnp.where(lost, ref.lost_two[come].astype(jnp.float32), two[to])
            w[to] = jnp.where(lost, ref.lost_w[come], w[to])
            return carry

        lax.fori_loop(0, 16, body, 0)

    state_first(W0)
    first((S1, GRADS), ALONG_Y, ref.grads_in, ref.grad_one)
    narrow(FIRST)
    state_first(ONE)
    narrow(SECOND)
    state_first(TWO0)
    tables()
    state_second(W0)
    state_first(TWO1)
    grad_second()
    state_second(ONE)
    state_back(W0)
    means_back()
    state_first(W1)
    state_down(W0)
    state_back(ONE)
    state_second(TWO0)
    means_down()
    state_second(W1)
    state_down(ONE)
    state_back(W1)
    state_back(TWO0)
    state_second(TWO1)
    state_down(W1)
    state_down(TWO0)
    swap_units(MEANS, 0, ref.half_mean)
    swap_units(ONE, 1, ref.half[FIRST])
    state_back(TWO1)
    survivors(0)
    state_down(TWO1)
    survivors(1)
    lost_weights(TWO0)
    lost_weights(TWO1)
    lost_state(TWO0)
    lost_state(TWO1)
    need(*pending)


def exchange(grads, state, maps):
    bf16, f32, i32 = jnp.bfloat16, jnp.float32, jnp.int32
    hbm, vmem = pl.BlockSpec(memory_space=pltpu.HBM), pl.BlockSpec(memory_space=pltpu.VMEM)
    vm = lambda shape, dtype=bf16, width=COLS: pltpu.VMEM(shape + (BAND, width), dtype)
    table = lambda size: pltpu.SMEM((size,), i32)
    whole = (2, 4, 2, 4)
    streams = lambda shape_of: tuple(vm(shape_of(axis), bf16, width) for _, axis, _, width in STREAMS)
    second = lambda axis: (4, 8 if axis == ALONG_X else HELD)
    final = (vm(whole), vm(whole, f32), vm(whole, f32))
    buffers = Buffers(
        grads_in=hbm, state_in=(hbm,) * 3, maps_in=(hbm,) * 4, final=final,
        narrow=(vm(whole), vm(whole)),
        grad_one=vm((17, 4)), grad_send=vm((4, HELD + 4)), grad_two=vm((4, HELD + 4)), mean=vm((LAYERS,), f32),
        mean_send=vm((4, HELD)), mean_back=vm((4, HELD)), mean_down=vm((4, 4, 2)), pair_down=vm((4, 4, 2)),
        half_mean=vm((4, 4, 2)), half=(vm((4, 4, 2)),) * 3,
        units=vm((2, 4, 2, 4, 2)), lost_two=vm((4, 2, 4, 2)), lost_w=vm((4, 2, 4, 2)),
        one=streams(lambda axis: (16, 4)), two_send=streams(second), two=streams(second),
        back_send=streams(lambda axis: (4, 4)), back=streams(lambda axis: (4, 4)),
        maps=tuple(pltpu.SMEM(array.shape, i32) for array in maps),
        pick=(table(8), table(HELD)), src=(table(LAYERS), table(LAYERS)), grad_at=table(4 * HELD), lost_at=table(4),
        sum_at=table(LAYERS), new_at=table(16), new_has=table(16), mean_at=table(8), unit_at=table(8), flags=table(3),
        sent=pltpu.SemaphoreType.DMA((37,)), got=pltpu.SemaphoreType.DMA((37,)),
    )
    leaves, tree = jax.tree.flatten(buffers)
    in_hbm = lambda array: pltpu.with_memory_space_constraint(array, pltpu.HBM)
    return pl.pallas_call(
        lambda *refs: exchange_kernel(tree, *refs),
        out_shape=final,
        in_specs=[hbm] * 8,
        out_specs=(vmem,) * 3,
        scratch_shapes=leaves[11:],
        compiler_params=pltpu.CompilerParams(collective_id=0, has_side_effects=True, vmem_limit_bytes=28 << 20),
        name="exchange",
    )(*[in_hbm(array.reshape(whole + (BAND, COLS))) for array in (grads, *state)], *[in_hbm(array) for array in maps])


def store_kernel(*refs):
    copies = []
    for at in range(3):
        src, dst = refs[at], refs[3 + at]
        for slot in range(2):
            for half in range(2):
                rows = pl.ds(half * 2, 2)
                copies.append(pltpu.make_async_copy(src.at[slot, rows], dst.at[slot, rows], refs[6].at[len(copies)]))
                copies[-1].start()
    for copy in copies:
        copy.wait()


def store(arrays):
    vmem, hbm = pl.BlockSpec(memory_space=pltpu.VMEM), pl.BlockSpec(memory_space=pltpu.HBM)
    return pl.pallas_call(
        store_kernel,
        out_shape=tuple(pltpu.HBM(array.shape, array.dtype) for array in arrays),
        in_specs=[vmem] * 3,
        out_specs=(hbm,) * 3,
        scratch_shapes=[pltpu.SemaphoreType.DMA((12,))],
        compiler_params=pltpu.CompilerParams(vmem_limit_bytes=8 << 20),
        name="store",
    )(*[pltpu.with_memory_space_constraint(array, pltpu.VMEM) for array in arrays])


def per_device(weights, first_moment, second_moment, gradients, old_section, new_section, lost_pipe, donor_offset):
    shape = weights.shape
    state = (weights, first_moment, second_moment)
    final = exchange(gradients, state, (old_section, new_section, lost_pipe, donor_offset))
    return tuple(array.reshape(shape) for array in store(final))


def solution(mesh):
    big, small = P("pipe", "section", None, "tp", None), P()
    return jax.shard_map(
        per_device,
        mesh=mesh,
        in_specs=(big, big, big, big, small, small, small, small),
        out_specs=(big, big, big),
        check_vma=False,
    )
```

time: 174 us -> 74.5 us (0.43); the launches traced: 172 us -> 74.4 us
  waiting for transfers between devices: 75.3 us -> 0 us
  Pallas kernels: 0 us -> 73.7 us
  local copies, waits for them, and re-layouts: 51.2 us -> 0 us
  starting transfers between devices: 32.6 us -> 0 us
  other arithmetic: 12.2 us -> 0 us
    all_to_all x7 -> x0, waiting for transfers between devices: 75.3 us -> none  [the longest x1 13.7 us: per_device(): lax.all_to_all(out_weight, ('pipe', 'section'), split_axis=0, concat_axis...]
    pallas_call x0 -> x2, Pallas kernels: none -> 73.7 us  [the longest x1 71.3 us: exchange(): pl.pallas_call(lambda *refs: exchange_kernel(tree, *refs), out_shape=fina...]
    all_to_all x7 -> x0, starting transfers between devices: 32.6 us -> none  [the longest x1 8.58 us: per_device(): lax.all_to_all(held_state[1].astype(jnp.bfloat16), ('pipe', 'section'), s...]
    scatter x3 -> x0, local copies, waits for them, and re-layouts: 16.4 us -> none  [the longest x1 6.25 us: per_device(): jnp.zeros(piece_weight.shape, jnp.bfloat16).at[place_index].set(next_weight)]
    unnamed x21 -> x0, local copies, waits for them, and re-layouts: 12.2 us -> none
    gather x9 -> x0, local copies, waits for them, and re-layouts: 10.2 us -> none  [the longest x1 2.75 us: per_device(): weight_now = piece_weight[source_index].astype(jnp.float32)]
    convert_element_type x9 -> x0, other arithmetic: 9.35 us -> none  [the longest x1 2.54 us: per_device(): next_weight = (weight_now - LEARN_RATE * update).astype(jnp.bfloat16)]
    all_to_all x7 -> x0, local copies, waits for them, and re-layouts: 5.32 us -> none  [the longest x2 2.46 us: per_device(): lax.all_to_all(held_state[0], ('pipe', 'section'), split_axis=1, concat_a...]
  transfers between devices with their start and end apart: 7 -> 0, of which waited for: 7 -> 0; matrix products, arithmetic and copies ran while one was open for 27% -> 0% of each run, Pallas kernels for 0% -> 0%
where the time goes in v2:
time: 74.5 us; the launch traced here: 74.4 us
  Pallas kernels  73.7 us (99%)
    pallas_call x1, Pallas kernels, exchange(): pl.pallas_call(lambda *refs: exchange_kernel(tree, *refs), out_shape=fina...  71.3 us
    pallas_call x1, Pallas kernels, store(): pl.pallas_call(store_kernel, out_shape=tuple((pltpu.HBM(array.shape, arra...  2.44 us

profile of v2, /device:TPU:1, one launch (start us, length us, event | category | flops | bytes accessed | tf_op | source)
XLA Modules:
  0.0 74.4 jit_solution(9786430839948901058)
XLA Ops:
  0.6 71.3 %exchange.1 = (bf16[2,4,2,4,16,512]{5,4,3,2,1,0:T(8,128)(2,1)S(1)}, f32[2,4,2,4,16,512]{5,4,3,2,1,0:T(8,128)S(1)}, f32[2,4,2,4,16,512]{5,4,3,2,1,0:T(8,128)S(1)}) custom-call(bf16[2,4,2,4,16,512]{5,4,3,2,1,0:T(8,128)(2,1)} %bitcast.9, bf16[2,4,2,4,16,512]{5,4,3,2,1,0:T(8,128)(2,1)} %bitcast.10, f32[2,4,2,4,16,512]{5,4,3,2,1,0:T(8,128)} %bitcast.7, ...), custom_call_target="tpu_custom_call" | custom-call | tf_op jit(solution)/shard_map/exchange/pallas_call | solution.py:477
  71.9 2.4 %store.1 = (bf16[2,4,2,4,16,512]{5,4,3,2,1,0:T(8,128)(2,1)}, f32[2,4,2,4,16,512]{5,4,3,2,1,0:T(8,128)}, f32[2,4,2,4,16,512]{5,4,3,2,1,0:T(8,128)}) custom-call(bf16[2,4,2,4,16,512]{5,4,3,2,1,0:T(8,128)(2,1)S(1)} %get-tuple-element.9.refs_0_, f32[2,4,2,4,16,512]{5,4,3,2,1,0:T(8,128)S(1)} %get-tuple-element.10.refs_1_, ...), custom_call_target="tpu_custom_call" | custom-call | tf_op jit(solution)/shard_map/store/pallas_call | solution.py:503

commit v3 on v2

--- a/solution.py
+++ b/solution.py
@@ -20,8 +20,8 @@
 WEIGHT, FIRST, SECOND = range(3)
 ALONG_X, ALONG_Y = range(2)
 STREAMS = (
-    (WEIGHT, ALONG_X, 0, 256),
-    (WEIGHT, ALONG_X, 256, 256),
+    (WEIGHT, ALONG_X, 0, 384),
+    (WEIGHT, ALONG_X, 384, 128),
     (FIRST, ALONG_X, 0, 512),
     (SECOND, ALONG_Y, 0, 384),
     (SECOND, ALONG_Y, 384, 128),
@@ -45,6 +45,9 @@
     state_in: Any
     maps_in: Any
     final: Any
+    lost_two: Any
+    lost_w: Any
+    flags: Any
     narrow: Any
     grad_one: Any
     grad_send: Any
@@ -54,11 +57,11 @@
     mean_back: Any
     mean_down: Any
     pair_down: Any
-    half_mean: Any
-    half: Any
     units: Any
-    lost_two: Any
-    lost_w: Any
+    half_w: Any
+    half_two: Any
+    far_w: Any
+    far_two: Any
     one: Any
     two_send: Any
     two: Any
@@ -74,7 +77,6 @@
     new_has: Any
     mean_at: Any
     unit_at: Any
-    flags: Any
     sent: Any
     got: Any
 
@@ -336,11 +338,12 @@
         need((R1, MEANS))
         for i in range(8):
             send[i // 2, :, i % 2] = got[:, ref.mean_at[i]]
-        down((R2, MEANS), lambda yy: send.at[yy], ref.half_mean)
+        down((R2, MEANS), lambda yy: send.at[yy], ref.units.at[0, :, c])
 
     def state_down(stream):
         array = STREAMS[stream][0]
-        got, dst = ref.back[stream], columns(stream, ref.half[array])
+        half = (ref.half_w, ref.units.at[1, :, c], ref.half_two)[array]
+        got, dst = ref.back[stream], columns(stream, half)
         need((R1, stream))
         if array != FIRST:
             down((R2, stream), lambda yy: got.at[:, pl.ds((yy % 2) * 2, 2)], dst)
@@ -352,12 +355,13 @@
             send[i // 2, :, i % 2] = jnp.where(at < HELD, layer, got[:, jnp.maximum(at - HELD, 0)])
         down((R2, stream), lambda yy: send.at[yy], dst)
 
-    def swap(key, src, dst):
-        begin(key, [(src, dst.at[:, c], device(y, x, 1 - c))], [(src, dst.at[:, c])], [dst], [src])
-
-    def swap_units(key, unit, src):
+    def swap(key, src, dst, landed):
+        begin(key, [(src, dst, device(y, x, 1 - c))], (), [landed], [src])
+
+    def swap_units(key, unit):
         need((R2, key))
-        swap((R3, key), src, ref.units.at[unit])
+        mine, other = ref.units.at[unit, :, c], ref.units.at[unit, :, 1 - c]
+        swap((R3, key), mine, mine, other)
 
     def survivors(slot):
         need((R3, MEANS), (R3, ONE), (LOAD, WEIGHT))
@@ -380,39 +384,37 @@
 
         lax.fori_loop(0, 32, body, 0, unroll=2)
 
-    def lost_weights(stream):
+    def swap_state(stream):
+        need((R2, stream))
+        src, dst = ((ref.half_w, ref.far_w) if STREAMS[stream][0] == WEIGHT else (ref.half_two, ref.far_two))
+        far = columns(stream, dst)
+        swap((R3, stream), columns(stream, src), far, far)
+
+    def lost_rows(stream, w, two, core):
+        start, width = STREAMS[stream][2:]
+        cols = slice(start, start + width)
+
+        def body(i, carry):
+            at = (i // 4, i % 4, slice(None), slice(None), cols)
+            weight, next_two = w[at].astype(jnp.float32), two[at].astype(jnp.float32)
+            next_one = ref.units[1, i // 4, core, i % 4, :, :, cols].astype(jnp.float32)
+            to = (slice(None), i // 4, core, i % 4, slice(None), cols)
+            ref.lost_w[to] = update(weight, next_one, next_two).astype(jnp.bfloat16)
+            ref.lost_two[to] = next_two
+            return carry
+
+        lax.fori_loop(0, 16, body, 0, unroll=2)
+
+    def lost_own(stream):
         need((R2, W0), (R2, W1), (R2, ONE), (R2, stream))
-        start, width = STREAMS[stream][2:]
-        w, one, two = ref.half
-
-        def body(i, carry):
-            at = (i // 4, i % 4, slice(None), slice(None), slice(start, start + width))
-            weight, next_one, next_two = [v[at].astype(jnp.float32) for v in (w, one, two)]
-            w[at] = update(weight, next_one, next_two).astype(jnp.bfloat16)
-            return carry
-
-        lax.fori_loop(0, 16, body, 0)
-        swap((R3, stream, SECOND), columns(stream, two), columns(stream, ref.lost_two))
-        swap((R3, stream, WEIGHT), columns(stream, w), columns(stream, ref.lost_w))
-
-    def lost_state(stream):
-        need((R3, stream, SECOND), (R3, stream, WEIGHT))
-        start, width = STREAMS[stream][2:]
-        w, _, two = ref.final
-        lost = ref.flags[0] == 1
-        cols = slice(start, start + width)
-
-        def body(i, carry):
-            slot, xb, cb = i // 8, (i // 2) % 4, i % 2
-            to, come = (slot, xb, cb, slice(None), slice(None), cols), (xb, cb, slice(None), slot, slice(None), cols)
-            two[to] = jnp.where(lost, ref.lost_two[come].astype(jnp.float32), two[to])
-            w[to] = jnp.where(lost, ref.lost_w[come], w[to])
-            return carry
-
-        lax.fori_loop(0, 16, body, 0)
-
+        lost_rows(stream, ref.half_w, ref.half_two, c)
+
+    def lost_far(stream):
+        need((R3, W0), (R3, W1), (R3, ONE), (R3, stream))
+        lost_rows(stream, ref.far_w, ref.far_two, 1 - c)
+
+    first((S1, GRADS), ALONG_Y, ref.grads_in, ref.grad_one)
     state_first(W0)
-    first((S1, GRADS), ALONG_Y, ref.grads_in, ref.grad_one)
     narrow(FIRST)
     state_first(ONE)
     narrow(SECOND)
@@ -430,22 +432,26 @@
     state_second(TWO0)
     means_down()
     state_second(W1)
+    swap_state(W0)
     state_down(ONE)
     state_back(W1)
     state_back(TWO0)
     state_second(TWO1)
     state_down(W1)
     state_down(TWO0)
-    swap_units(MEANS, 0, ref.half_mean)
-    swap_units(ONE, 1, ref.half[FIRST])
+    swap_units(MEANS, 0)
+    swap_units(ONE, 1)
     state_back(TWO1)
     survivors(0)
+    swap_state(W1)
     state_down(TWO1)
     survivors(1)
-    lost_weights(TWO0)
-    lost_weights(TWO1)
-    lost_state(TWO0)
-    lost_state(TWO1)
+    swap_state(TWO0)
+    lost_own(TWO0)
+    swap_state(TWO1)
+    lost_own(TWO1)
+    lost_far(TWO0)
+    lost_far(TWO1)
     need(*pending)
 
 
@@ -458,64 +464,87 @@
     streams = lambda shape_of: tuple(vm(shape_of(axis), bf16, width) for _, axis, _, width in STREAMS)
     second = lambda axis: (4, 8 if axis == ALONG_X else HELD)
     final = (vm(whole), vm(whole, f32), vm(whole, f32))
+    outputs = final + (vm(whole, f32), vm(whole), table(3))
     buffers = Buffers(
-        grads_in=hbm, state_in=(hbm,) * 3, maps_in=(hbm,) * 4, final=final,
+        grads_in=hbm, state_in=(hbm,) * 3, maps_in=(hbm,) * 4,
+        final=final, lost_two=outputs[3], lost_w=outputs[4], flags=outputs[5],
         narrow=(vm(whole), vm(whole)),
         grad_one=vm((17, 4)), grad_send=vm((4, HELD + 4)), grad_two=vm((4, HELD + 4)), mean=vm((LAYERS,), f32),
         mean_send=vm((4, HELD)), mean_back=vm((4, HELD)), mean_down=vm((4, 4, 2)), pair_down=vm((4, 4, 2)),
-        half_mean=vm((4, 4, 2)), half=(vm((4, 4, 2)),) * 3,
-        units=vm((2, 4, 2, 4, 2)), lost_two=vm((4, 2, 4, 2)), lost_w=vm((4, 2, 4, 2)),
+        units=vm((2, 4, 2, 4, 2)), half_w=vm((4, 4, 2)), half_two=vm((4, 4, 2)), far_w=vm((4, 4, 2)), far_two=vm((4, 4, 2)),
         one=streams(lambda axis: (16, 4)), two_send=streams(second), two=streams(second),
         back_send=streams(lambda axis: (4, 4)), back=streams(lambda axis: (4, 4)),
         maps=tuple(pltpu.SMEM(array.shape, i32) for array in maps),
         pick=(table(8), table(HELD)), src=(table(LAYERS), table(LAYERS)), grad_at=table(4 * HELD), lost_at=table(4),
-        sum_at=table(LAYERS), new_at=table(16), new_has=table(16), mean_at=table(8), unit_at=table(8), flags=table(3),
+        sum_at=table(LAYERS), new_at=table(16), new_has=table(16), mean_at=table(8), unit_at=table(8),
         sent=pltpu.SemaphoreType.DMA((37,)), got=pltpu.SemaphoreType.DMA((37,)),
     )
     leaves, tree = jax.tree.flatten(buffers)
     in_hbm = lambda array: pltpu.with_memory_space_constraint(array, pltpu.HBM)
     return pl.pallas_call(
         lambda *refs: exchange_kernel(tree, *refs),
-        out_shape=final,
+        out_shape=outputs[:5] + (jax.ShapeDtypeStruct((3,), i32),),
         in_specs=[hbm] * 8,
-        out_specs=(vmem,) * 3,
-        scratch_shapes=leaves[11:],
+        out_specs=(vmem,) * 5 + (pl.BlockSpec(memory_space=pltpu.SMEM),),
+        scratch_shapes=leaves[14:],
         compiler_params=pltpu.CompilerParams(collective_id=0, has_side_effects=True, vmem_limit_bytes=28 << 20),
         name="exchange",
     )(*[in_hbm(array.reshape(whole + (BAND, COLS))) for array in (grads, *state)], *[in_hbm(array) for array in maps])
 
 
-def store_kernel(*refs):
-    copies = []
-    for at in range(3):
-        src, dst = refs[at], refs[3 + at]
+def store_kernel(w, one, two, lost_two, lost_w, flags_in, out_w, out_one, out_two, flags, flag_sem, sem):
+    load = pltpu.make_async_copy(flags_in, flags, flag_sem)
+    load.start()
+
+    def pieces(src, dst, at):
+        copies = []
         for slot in range(2):
             for half in range(2):
                 rows = pl.ds(half * 2, 2)
-                copies.append(pltpu.make_async_copy(src.at[slot, rows], dst.at[slot, rows], refs[6].at[len(copies)]))
-                copies[-1].start()
-    for copy in copies:
+                copies.append(pltpu.make_async_copy(src.at[slot, rows], dst.at[slot, rows], sem.at[at + len(copies)]))
+        return copies
+
+    first = pieces(one, out_one, 0)
+    for copy in first:
+        copy.start()
+    load.wait()
+    held = pieces(two, out_two, 4) + pieces(w, out_w, 8)
+    come = pieces(lost_two, out_two, 4) + pieces(lost_w, out_w, 8)
+
+    @pl.when(flags[0] == 0)
+    def _():
+        for copy in held:
+            copy.start()
+
+    @pl.when(flags[0] == 1)
+    def _():
+        for copy in come:
+            copy.start()
+
+    for copy in first + held:
         copy.wait()
 
 
-def store(arrays):
+def store(arrays, flags):
     vmem, hbm = pl.BlockSpec(memory_space=pltpu.VMEM), pl.BlockSpec(memory_space=pltpu.HBM)
     return pl.pallas_call(
         store_kernel,
-        out_shape=tuple(pltpu.HBM(array.shape, array.dtype) for array in arrays),
-        in_specs=[vmem] * 3,
+        out_shape=tuple(pltpu.HBM(array.shape, array.dtype) for array in arrays[:3]),
+        in_specs=[vmem] * 5 + [pl.BlockSpec(memory_space=pl.ANY)],
         out_specs=(hbm,) * 3,
-        scratch_shapes=[pltpu.SemaphoreType.DMA((12,))],
+        scratch_shapes=[
+            pltpu.SMEM(flags.shape, flags.dtype), pltpu.SemaphoreType.DMA, pltpu.SemaphoreType.DMA((12,)),
+        ],
         compiler_params=pltpu.CompilerParams(vmem_limit_bytes=8 << 20),
         name="store",
-    )(*[pltpu.with_memory_space_constraint(array, pltpu.VMEM) for array in arrays])
+    )(*[pltpu.with_memory_space_constraint(array, pltpu.VMEM) for array in arrays], flags)
 
 
 def per_device(weights, first_moment, second_moment, gradients, old_section, new_section, lost_pipe, donor_offset):
     shape = weights.shape
     state = (weights, first_moment, second_moment)
     final = exchange(gradients, state, (old_section, new_section, lost_pipe, donor_offset))
-    return tuple(array.reshape(shape) for array in store(final))
+    return tuple(array.reshape(shape) for array in store(final[:5], final[5]))
 
 
 def solution(mesh):

time: 74.5 us -> 73.2 us (0.983)
  Pallas kernels: 73.7 us -> 72.5 us
    pallas_call x1, Pallas kernels: 71.3 us -> 70.1 us  [exchange(): pl.pallas_call(lambda *refs: exchange_kernel(tree, *refs), out_shape=outp...]
where the time goes in v3:
time: 73.2 us
  Pallas kernels  72.5 us (99%)
    pallas_call x1, Pallas kernels, exchange(): pl.pallas_call(lambda *refs: exchange_kernel(tree, *refs), out_shape=outp...  70.1 us
    pallas_call x1, Pallas kernels, store(): pl.pallas_call(store_kernel, out_shape=tuple((pltpu.HBM(array.shape, arra...  2.44 us

profile of v3, /device:TPU:1, one launch (start us, length us, event | category | flops | bytes accessed | tf_op | source)
XLA Modules:
  0.0 73.2 jit_solution(6140256669448643478)
XLA Ops:
  0.6 70.1 %exchange.1 = (bf16[2,4,2,4,16,512]{5,4,3,2,1,0:T(8,128)(2,1)S(1)}, f32[2,4,2,4,16,512]{5,4,3,2,1,0:T(8,128)S(1)}, f32[2,4,2,4,16,512]{5,4,3,2,1,0:T(8,128)S(1)}...) custom-call(bf16[2,4,2,4,16,512]{5,4,3,2,1,0:T(8,128)(2,1)} %bitcast.9, ...), custom_call_target="tpu_custom_call" | custom-call | tf_op jit(solution)/shard_map/exchange/pallas_call | solution.py:484
  70.7 2.4 %store.1 = (bf16[2,4,2,4,16,512]{5,4,3,2,1,0:T(8,128)(2,1)}, f32[2,4,2,4,16,512]{5,4,3,2,1,0:T(8,128)}, f32[2,4,2,4,16,512]{5,4,3,2,1,0:T(8,128)}) custom-call(bf16[2,4,2,4,16,512]{5,4,3,2,1,0:T(8,128)(2,1)S(1)} %get-tuple-element.12.w, f32[2,4,2,4,16,512]{5,4,3,2,1,0:T(8,128)S(1)} %get-tuple-element.13.one, ...), custom_call_target="tpu_custom_call" | custom-call | tf_op jit(solution)/shard_map/store/pallas_call | solution.py:530

commit v4 on v3

--- a/solution.py
+++ b/solution.py
@@ -99,7 +99,7 @@
     y = (pipe // 2) * 2 + section // 4
     x = section % 4
     c = pipe % 2
-    ring = (1, 3, 2)
+    ring = (2, 1, 3)
     with_core = [(step, dc) for step in ring for dc in (0, 1)] + [(0, 1)]
     pending = {}
 
@@ -499,8 +499,8 @@
     def pieces(src, dst, at):
         copies = []
         for slot in range(2):
-            for half in range(2):
-                rows = pl.ds(half * 2, 2)
+            for quarter in range(4):
+                rows = pl.ds(quarter, 1)
                 copies.append(pltpu.make_async_copy(src.at[slot, rows], dst.at[slot, rows], sem.at[at + len(copies)]))
         return copies
 
@@ -508,8 +508,8 @@
     for copy in first:
         copy.start()
     load.wait()
-    held = pieces(two, out_two, 4) + pieces(w, out_w, 8)
-    come = pieces(lost_two, out_two, 4) + pieces(lost_w, out_w, 8)
+    held = pieces(two, out_two, 8) + pieces(w, out_w, 16)
+    come = pieces(lost_two, out_two, 8) + pieces(lost_w, out_w, 16)
 
     @pl.when(flags[0] == 0)
     def _():
@@ -533,7 +533,7 @@
         in_specs=[vmem] * 5 + [pl.BlockSpec(memory_space=pl.ANY)],
         out_specs=(hbm,) * 3,
         scratch_shapes=[
-            pltpu.SMEM(flags.shape, flags.dtype), pltpu.SemaphoreType.DMA, pltpu.SemaphoreType.DMA((12,)),
+            pltpu.SMEM(flags.shape, flags.dtype), pltpu.SemaphoreType.DMA, pltpu.SemaphoreType.DMA((24,)),
         ],
         compiler_params=pltpu.CompilerParams(vmem_limit_bytes=8 << 20),
         name="store",

time: 73.2 us -> 73.6 us (level)
  no operation moved by 1% of the time
where the time goes in v4:
time: 73.6 us; the launch traced here: 73.5 us
  Pallas kernels  72.9 us (99%)
    pallas_call x1, Pallas kernels, exchange(): pl.pallas_call(lambda *refs: exchange_kernel(tree, *refs), out_shape=outp...  70.4 us
    pallas_call x1, Pallas kernels, store(): pl.pallas_call(store_kernel, out_shape=tuple((pltpu.HBM(array.shape, arra...  2.53 us

profile of v4, /device:TPU:1, one launch (start us, length us, event | category | flops | bytes accessed | tf_op | source)
XLA Modules:
  0.0 73.5 jit_solution(111447975480905610)
XLA Ops:
  0.6 70.4 %exchange.1 = (bf16[2,4,2,4,16,512]{5,4,3,2,1,0:T(8,128)(2,1)S(1)}, f32[2,4,2,4,16,512]{5,4,3,2,1,0:T(8,128)S(1)}, f32[2,4,2,4,16,512]{5,4,3,2,1,0:T(8,128)S(1)}...) custom-call(bf16[2,4,2,4,16,512]{5,4,3,2,1,0:T(8,128)(2,1)} %bitcast.9, ...), custom_call_target="tpu_custom_call" | custom-call | tf_op jit(solution)/shard_map/exchange/pallas_call | solution.py:484
  71.0 2.5 %store.1 = (bf16[2,4,2,4,16,512]{5,4,3,2,1,0:T(8,128)(2,1)}, f32[2,4,2,4,16,512]{5,4,3,2,1,0:T(8,128)}, f32[2,4,2,4,16,512]{5,4,3,2,1,0:T(8,128)}) custom-call(bf16[2,4,2,4,16,512]{5,4,3,2,1,0:T(8,128)(2,1)S(1)} %get-tuple-element.12.w, f32[2,4,2,4,16,512]{5,4,3,2,1,0:T(8,128)S(1)} %get-tuple-element.13.one, ...), custom_call_target="tpu_custom_call" | custom-call | tf_op jit(solution)/shard_map/store/pallas_call | solution.py:530
